TPU v7x, 128 devices: a whole 4x4x4 slice. The times are simulated.
128 devices in a mesh: gx: 4 (over x), gy: 32 (over z, y, core).
Axes of the slice: x: 4, y: 4, z: 4, core: 2. Of those that a mesh axis runs over, the one named last changes fastest.
Arguments:
- starting_sag: float32 [512, 4096], P('gx', 'gy'), may hold values from -6 to 6
- warmth_celsius_field: float32 [512, 4096], P('gx', 'gy'), may hold values from 25 to 125
- junction_charge_store: float32 [512, 4096], P('gx', 'gy'), may hold values from 5e-05 to 0.0005
- load_amperes: float32 [2, 512, 4096], P(None, 'gx', 'gy'), may hold values from -0.08 to 0.08
- source_patch_bits: int32 [16, 128], P('gx', 'gy'), may hold values 0 or 1
Outputs:
- drop: float32 [512, 4096], P('gx', 'gy')
All inputs are finite; a program needn't handle non-finite values. No bound on the sum of `source_patch_bits` on one device may be relied on, other than what follows from the above.
Results may differ from a plain program's by a relative error of at most 0.0013.
Values sent between devices are 32-bit elements; how exact they have to be, the bound alone decides.
No kernel may reach another device: no remote copies, remote signals or barrier semaphores. Data moves between devices by JAX's collectives and lax.ppermute only.
A program may use at most 64 MiB of HBM per device.

v0:
```python
import jax
import jax.numpy as jnp
from jax import lax
from jax.sharding import PartitionSpec as P

STEPS = 2
PITCH = 32


xward_admittance = 1.0
yward_admittance = 0.5
warmth_scaling = 0.004
surrounding_warmth = 25.0
cushion_pieces = 1.0


def with_halo(x, sides, width):
    for axis, dim in sides:
        devices, length = (lax.axis_size(axis), x.shape[dim])
        up = [(i, (i + 1) % devices) for i in range(devices - 1)]
        down = [(j, i) for i, j in up]
        last = lax.slice_in_dim(x, length - width, length, axis=dim)
        first = lax.slice_in_dim(x, 0, width, axis=dim)
        before = lax.ppermute(last, axis, up)
        after = lax.ppermute(first, axis, down)
        x = jnp.concatenate([before, x, after], axis=dim)
    return x


def factor(sub_diag, main_diag, sup_diag):

    def advance(prev_ratio, packed):
        sub_row, main_row, sup_row = packed
        pivot_row = 1.0 / (main_row - sub_row * prev_ratio)
        next_ratio = sup_row * pivot_row
        return (next_ratio, (pivot_row, next_ratio))

    _, (pivots, ratios) = lax.scan(
        advance, jnp.zeros_like(main_diag[0]), (sub_diag, main_diag, sup_diag)
    )
    return (pivots, ratios)


def substitute(sub_diag, pivots, ratios, source):

    def forward(prev_value, packed):
        sub_row, pivot_row, source_row = packed
        new_value = (source_row - sub_row * prev_value) * pivot_row
        return (new_value, new_value)

    _, partial_sol = lax.scan(forward, jnp.zeros_like(source[0]), (sub_diag, pivots, source))

    def backward(next_value, packed):
        ratio_row, partial_row = packed
        new_value = partial_row - ratio_row * next_value
        return (new_value, new_value)

    _, solved = lax.scan(backward, jnp.zeros_like(source[0]), (ratios, partial_sol), reverse=True)
    return solved


def spike_pair(lower, upper, pivots, ratios):
    length = lower.shape[0]
    row_ids = jnp.arange(length)[:, None]
    spike_upper = jnp.where(row_ids == length - 1, upper[-1][None, :], 0.0)
    spike_lower = jnp.where(row_ids == 0, lower[0][None, :], 0.0)
    spikes = substitute(-lower, pivots, ratios, jnp.stack([spike_upper, spike_lower], 1))
    return (spikes[:, 0], spikes[:, 1])


def relation(local_sol, reach_next, reach_prev):
    return jnp.stack(
        [local_sol[0], local_sol[-1], reach_next[0], reach_next[-1], reach_prev[0], reach_prev[-1]]
    )


def join(left_part, right_part):
    scaled = 1.0 / (1.0 - left_part[3] * right_part[4])
    last_base = (left_part[1] + left_part[3] * right_part[0]) * scaled
    last_right = left_part[3] * right_part[2] * scaled
    last_left = left_part[5] * scaled
    first_base = right_part[0] + right_part[4] * last_base
    first_right = right_part[2] + right_part[4] * last_right
    first_left = right_part[4] * last_left
    return jnp.stack(
        [
            left_part[0] + left_part[2] * first_base,
            right_part[1] + right_part[5] * last_base,
            left_part[2] * first_right,
            right_part[3] + right_part[5] * last_right,
            left_part[4] + left_part[2] * first_left,
            right_part[5] * last_left,
        ]
    )


def junction(left_part, right_part):
    scaled = 1.0 / (1.0 - left_part[3] * right_part[4])
    last_base = (left_part[1] + left_part[3] * right_part[0]) * scaled
    return (last_base, right_part[0] + right_part[4] * last_base)


def every_side(gathered, identity):

    def extend_left(running, member):
        return (join(running, member), running)

    _, prefix = lax.scan(extend_left, identity, gathered)

    def extend_right(running, member):
        return (join(member, running), running)

    _, suffix = lax.scan(extend_right, identity, gathered, reverse=True)
    return (prefix, suffix)


def finish(local_sol, own_rel, from_left, from_right, reach_next, reach_prev):
    left_last, _ = junction(from_left, join(own_rel, from_right))
    _, right_first = junction(join(from_left, own_rel), from_right)
    return local_sol + reach_next * right_first + reach_prev * left_last


def unit_relation(width):
    return jnp.broadcast_to(
        jnp.array([0.0, 0.0, 1.0, 0.0, 0.0, 1.0], jnp.float32)[:, None], (6, width)
    )


def local(
    starting_sag, warmth_celsius_field, junction_charge_store, load_amperes, source_patch_bits
):
    rows_dev, cols_dev = starting_sag.shape
    count_x = lax.axis_size("gx")
    count_y = lax.axis_size("gy")
    place_x = lax.axis_index("gx")
    place_y = lax.axis_index("gy")
    width_col = rows_dev // count_y
    rim_allowance = with_halo(warmth_celsius_field, (("gx", 0), ("gy", 1)), 1)
    inner_x = rim_allowance[:, 1:-1]
    xward_wire = xward_admittance / (
        1.0 + warmth_scaling * (0.5 * (inner_x[:-1] + inner_x[1:]) - surrounding_warmth)
    )
    row_pos = jnp.arange(rows_dev + 1)[:, None]
    outside_x = (place_x == 0) & (row_pos == 0) | (place_x == count_x - 1) & (row_pos == rows_dev)
    xward_wire = jnp.where(outside_x, 0.0, xward_wire)
    inner_y = rim_allowance[1:-1]
    yward_wire = yward_admittance / (
        1.0 + warmth_scaling * (0.5 * (inner_y[:, :-1] + inner_y[:, 1:]) - surrounding_warmth)
    )
    col_pos = jnp.arange(cols_dev + 1)[None, :]
    outside_y = (place_y == 0) & (col_pos == 0) | (place_y == count_y - 1) & (col_pos == cols_dev)
    yward_wire = jnp.where(outside_y, 0.0, yward_wire)
    left_x = xward_wire[:-1]
    right_x = xward_wire[1:]
    left_y = yward_wire[:, :-1]
    right_y = yward_wire[:, 1:]
    flag_vals = source_patch_bits.astype(jnp.float32)
    first_pos = (jnp.arange(PITCH) == 0).astype(jnp.float32)
    semi_cushion = cushion_pieces * (
        flag_vals[:, None, :, None]
        * first_pos[None, :, None, None]
        * first_pos[None, None, None, :]
    ).reshape(rows_dev, cols_dev)
    diag_x = junction_charge_store + left_x + right_x + semi_cushion
    pivots_x, ratios_x = factor(-left_x, diag_x, -right_x)
    reach_right, reach_left = spike_pair(left_x, right_x, pivots_x, ratios_x)
    cap_col, pad_col, lower_col, upper_col = (
        lax.all_to_all(junction_charge_store.T, "gy", split_axis=1, concat_axis=1, tiled=True),
        lax.all_to_all(semi_cushion.T, "gy", split_axis=1, concat_axis=1, tiled=True),
        lax.all_to_all(left_y.T, "gy", split_axis=1, concat_axis=1, tiled=True),
        lax.all_to_all(right_y.T, "gy", split_axis=1, concat_axis=1, tiled=True),
    )
    diag_col = cap_col + lower_col + upper_col + pad_col
    pivots_y, ratios_y = factor(-lower_col, diag_col, -upper_col)
    reach_up, reach_down = spike_pair(lower_col, upper_col, pivots_y, ratios_y)
    identity = unit_relation(cols_dev)
    block_identity = unit_relation(width_col)
    drop_now = starting_sag
    for step_index in range(STEPS):
        padded = with_halo(drop_now, (("gy", 1),), 1)
        source = (
            junction_charge_store * drop_now
            - (
                right_y * (drop_now - padded[:, 2:])
                + left_y * (drop_now - padded[:, :-2])
                + semi_cushion * drop_now
            )
            + load_amperes[step_index]
        )
        solve_local_sol = substitute(-left_x, pivots_x, ratios_x, source)
        solve_own_rel = relation(solve_local_sol, reach_right, reach_left)
        gathered = lax.all_gather(solve_own_rel[None], "gx", axis=0, tiled=True)
        solve_prefix, solve_suffix = every_side(gathered, identity)
        from_left = lax.dynamic_index_in_dim(solve_prefix, place_x, 0, False)
        from_right = lax.dynamic_index_in_dim(solve_suffix, place_x, 0, False)
        half_drop = finish(
            solve_local_sol, solve_own_rel, from_left, from_right, reach_right, reach_left
        )
        operate_padded = with_halo(half_drop, (("gx", 0),), 1)
        source = (
            junction_charge_store * half_drop
            - (
                right_x * (half_drop - operate_padded[2:])
                + left_x * (half_drop - operate_padded[:-2])
                + semi_cushion * half_drop
            )
            + load_amperes[step_index]
        )
        column_src = lax.all_to_all(source.T, "gy", split_axis=1, concat_axis=1, tiled=True)
        local_sol = substitute(-lower_col, pivots_y, ratios_y, column_src)
        own_rel = relation(local_sol, reach_up, reach_down)
        blocks = own_rel.reshape(6, count_y, width_col).transpose(1, 0, 2)
        prefix, suffix = every_side(blocks, block_identity)
        from_low = prefix.transpose(1, 0, 2).reshape(6, rows_dev)
        from_high = suffix.transpose(1, 0, 2).reshape(6, rows_dev)
        column_drop = finish(local_sol, own_rel, from_low, from_high, reach_up, reach_down)
        line_drop = lax.all_to_all(column_drop, "gy", split_axis=1, concat_axis=1, tiled=True).T
        drop_now = line_drop
    return drop_now


def solution(mesh):
    return jax.shard_map(
        local,
        mesh=mesh,
        in_specs=(P("gx", "gy"), P("gx", "gy"), P("gx", "gy"), P(None, "gx", "gy"), P("gx", "gy")),
        out_specs=P("gx", "gy"),
        check_vma=False,
    )
```

profile of v0, /device:TPU:1, one launch (start us, length us, event | category | flops | bytes accessed | tf_op | source)
XLA Modules:
  0.0 334.7 jit_solution(12870772982030978133)
XLA Ops:
  20.9 14.5 %while.330 = (s32[]{:T(128)}, f32[128]{0:T(128)S(1)}, f32[128,128]{1,0:T(8,128)S(1)}, f32[128,128]{1,0:T(8,128)S(1)}, f32[128,128]{1,0:T(8,128)S(1)}, /*index=5*...) while((s32[]{:T(128)}, f32[128]{0:T(128)S(1)}, f32[128,128]{1,0:T(8,128)S(1)}, ...), condition=%wide.region_3.4_spmd.clone, body=%wide.region_2.3_spmd.clone.sunk | while | flops 643 | bytes 5235 | solution.py:38
  38.0 9.6 %all-to-all-start.2 = ((f32[128,32,4]{0,2,1:T(4,128)}), f32[128,32,4]{0,2,1:T(4,128)S(1)}, u32[]{:S(2)}, u32[]{:S(2)}) async-start(f32[128,32,4]{0,2,1:T(4,128)} %bitcast.79), calls=%async_computation.2 | async-start | bytes 131072 | tf_op jit(solution)/shard_map/all_to_all | solution.py:171
  47.7 9.6 %while.331 = (s32[]{:T(128)}, f32[128]{0:T(128)S(1)}, f32[128,128]{1,0:T(8,128)S(1)}, f32[128,128]{1,0:T(8,128)S(1)}, f32[128,128]{1,0:T(8,128)S(1)}, /*index=5*/f32[128,128]{1,0:T(8,128)S(1)}, s32[]{:T(128)}, s32[]{:T(128)}) while((s32[]{:T(128)}, f32[128]{0:T(128)S(1)}, f32[128,128]{1,0:T(8,128)S(1)}, f32[128,128]{1,0:T(8,128)S(1)}, ...), condition=%wide.region_5.6_spmd.clone, body=%wide.region_4.5_spmd.clone.sunk | while | flops 515 | bytes 3687 | solution.py:51
  57.3 9.6 %while.332 = (s32[]{:T(128)}, f32[128]{0:T(128)S(1)}, f32[128,128]{1,0:T(8,128)S(1)}, f32[128,128]{1,0:T(8,128)S(1)}, f32[128,128]{1,0:T(8,128)S(1)}, /*index=5*/s32[]{:T(128)}, s32[]{:T(128)}, s32[]{:T(128)}) while((s32[]{:T(128)}, f32[128]{0:T(128)S(1)}, f32[128,128]{1,0:T(8,128)S(1)}, f32[128,128]{1,0:T(8,128)S(1)}, ...), condition=%wide.region_7.8_spmd.clone, body=%wide.region_6.7_spmd.clone.sunk | while | flops 388 | bytes 3187 | solution.py:58
  67.0 7.4 %all-to-all-start.1 = ((f32[128,32,4]{0,2,1:T(4,128)}), f32[128,32,4]{0,2,1:T(4,128)S(1)}, u32[]{:S(2)}, u32[]{:S(2)}) async-start(f32[128,32,4]{0,2,1:T(4,128)} %bitcast.76), calls=%async_computation.1 | async-start | bytes 131072 | tf_op jit(solution)/shard_map/all_to_all | solution.py:170
  74.7 7.0 %all-to-all-done.1 = f32[128,32,4]{0,2,1:T(4,128)S(1)} async-done(((f32[128,32,4]{0,2,1:T(4,128)}), f32[128,32,4]{0,2,1:T(4,128)S(1)}, u32[]{:S(2)}, u32[]{:S(2)}) %all-to-all-start.1) | async-done | bytes 65568 | tf_op jit(solution)/shard_map/all_to_all | solution.py:170
  86.4 7.3 %while.333 = (s32[]{:T(128)}, f32[2,128]{1,0:T(2,128)S(1)}, f32[128,2,128]{2,1,0:T(2,128)S(1)}, f32[128,2,128]{2,1,0:T(2,128)S(1)}, f32[128,128]{1,0:T(8,128)S(1...) while((s32[]{:T(128)}, f32[2,128]{1,0:T(2,128)S(1)}, f32[128,2,128]{2,1,0:T(2,128)S(1)}, ...), condition=%wide.region_9.10_spmd.clone, body=%wide.region_8.9_spmd.clone.sunk | while | flops 1027 | bytes 7271 | solution.py:51
  93.8 7.1 %while.334 = (s32[]{:T(128)}, f32[2,128]{1,0:T(2,128)S(1)}, f32[128,2,128]{2,1,0:T(2,128)S(1)}, f32[128,2,128]{2,1,0:T(2,128)S(1)}, f32[128,128]{1,0:T(8,128)S(1)}, /*index=5*/s32[]{:T(128)}, s32[]{:T(128)}, s32[]{:T(128)}) while((s32[]{:T(128)}, f32[2,128]{1,0:T(2,128)S(1)}, f32[128,2,128]{2,1,0:T(2,128)S(1)}, ...), condition=%wide.region_11.12_spmd.clone, body=%wide.region_10.11_spmd.clone.sunk | while | flops 772 | bytes 5747 | solution.py:58
  101.0 10.3 %all-gather.2 = f32[4,6,128]{2,1,0:T(8,128)S(1)} all-gather(f32[1,6,128]{2,1,0:T(8,128)S(1)} %bitcast.1283), channel_id=2, replica_groups=mesh['gx'=4,'gy'=32] {'gx'}, dimensions={0}, use_global_device_ids=true | all-gather | bytes 15360 | tf_op jit(solution)/shard_map/all_gather | solution.py:192
  112.9 10.4 %all-to-all-start.4 = ((f32[128,32,4]{0,2,1:T(4,128)}), f32[128,32,4]{0,2,1:T(4,128)S(1)}, u32[]{:S(2)}, u32[]{:S(2)}) async-start(f32[128,32,4]{0,2,1:T(4,128)} %bitcast.84), calls=%async_computation.4 | async-start | bytes 131072 | tf_op jit(solution)/shard_map/all_to_all | solution.py:169
  123.3 7.3 %all-to-all-done.4 = f32[128,32,4]{0,2,1:T(4,128)S(1)} async-done(((f32[128,32,4]{0,2,1:T(4,128)}), f32[128,32,4]{0,2,1:T(4,128)S(1)}, u32[]{:S(2)}, u32[]{:S(2)}) %all-to-all-start.4) | async-done | bytes 65568 | tf_op jit(solution)/shard_map/all_to_all | solution.py:169
  131.0 14.5 %while.335 = (s32[]{:T(128)}, f32[128]{0:T(128)S(1)}, f32[128,128]{1,0:T(8,128)S(1)}, f32[128,128]{1,0:T(8,128)S(1)}, f32[128,128]{1,0:T(8,128)S(1)}, /*index=5*...) while((s32[]{:T(128)}, f32[128]{0:T(128)S(1)}, f32[128,128]{1,0:T(8,128)S(1)}, ...), condition=%wide.region_1.2_spmd.clone, body=%wide.region_0.1_spmd.clone.sunk | while | flops 643 | bytes 5235 | solution.py:38
  151.0 7.3 %while.338 = (s32[]{:T(128)}, f32[2,128]{1,0:T(2,128)S(1)}, f32[128,2,128]{2,1,0:T(2,128)S(1)}, f32[128,2,128]{2,1,0:T(2,128)S(1)}, f32[128,128]{1,0:T(8,128)S(1...) while((s32[]{:T(128)}, f32[2,128]{1,0:T(2,128)S(1)}, f32[128,2,128]{2,1,0:T(2,128)S(1)}, ...), condition=%wide.region_21.22_spmd.clone, body=%wide.region_20.21_spmd.clone.sunk | while | flops 1027 | bytes 7271 | solution.py:51
  158.4 7.1 %while.339 = (s32[]{:T(128)}, f32[2,128]{1,0:T(2,128)S(1)}, f32[128,2,128]{2,1,0:T(2,128)S(1)}, f32[128,2,128]{2,1,0:T(2,128)S(1)}, f32[128,128]{1,0:T(8,128)S(1)}, /*index=5*/s32[]{:T(128)}, s32[]{:T(128)}, s32[]{:T(128)}) while((s32[]{:T(128)}, f32[2,128]{1,0:T(2,128)S(1)}, f32[128,2,128]{2,1,0:T(2,128)S(1)}, ...), condition=%wide.region_23.24_spmd.clone, body=%wide.region_22.23_spmd.clone.sunk | while | flops 772 | bytes 5747 | solution.py:58
  167.2 4.5 %all-to-all-start = ((f32[128,32,4]{0,2,1:T(4,128)}), f32[128,32,4]{0,2,1:T(4,128)S(1)}, u32[]{:S(2)}, u32[]{:S(2)}) async-start(f32[128,32,4]{0,2,1:T(4,128)} %bitcast.73), calls=%async_computation | async-start | bytes 131072 | tf_op jit(solution)/shard_map/all_to_all | solution.py:209
  172.4 6.7 %all-to-all-done = f32[128,32,4]{0,2,1:T(4,128)S(1)} async-done(((f32[128,32,4]{0,2,1:T(4,128)}), f32[128,32,4]{0,2,1:T(4,128)S(1)}, u32[]{:S(2)}, u32[]{:S(2)}) %all-to-all-start) | async-done | bytes 65568 | tf_op jit(solution)/shard_map/all_to_all | solution.py:209
  179.2 9.6 %while.336 = (s32[]{:T(128)}, f32[128]{0:T(128)S(1)}, f32[128,128]{1,0:T(8,128)S(1)}, f32[128,128]{1,0:T(8,128)S(1)}, f32[128,128]{1,0:T(8,128)S(1)}, /*index=5*/f32[128,128]{1,0:T(8,128)S(1)}, s32[]{:T(128)}, s32[]{:T(128)}) while((s32[]{:T(128)}, f32[128]{0:T(128)S(1)}, f32[128,128]{1,0:T(8,128)S(1)}, ...), condition=%wide.region_17.18_spmd.clone, body=%wide.region_16.17_spmd.clone.sunk | while | flops 515 | bytes 3687 | solution.py:51
  188.8 9.6 %while.337 = (s32[]{:T(128)}, f32[128]{0:T(128)S(1)}, f32[128,128]{1,0:T(8,128)S(1)}, f32[128,128]{1,0:T(8,128)S(1)}, f32[128,128]{1,0:T(8,128)S(1)}, /*index=5*/s32[]{:T(128)}, s32[]{:T(128)}, s32[]{:T(128)}) while((s32[]{:T(128)}, f32[128]{0:T(128)S(1)}, f32[128,128]{1,0:T(8,128)S(1)}, f32[128,128]{1,0:T(8,128)S(1)}, ...), condition=%wide.region_19.20_spmd.clone, body=%wide.region_18.19_spmd.clone.sunk | while | flops 388 | bytes 3187 | solution.py:58
  199.3 6.7 %while.325 = (s32[]{:T(128)}, f32[6,4]{1,0:T(8,128)S(1)}, f32[32,6,4]{1,2,0:T(4,128)S(1)}, f32[32,6,4]{2,1,0:T(8,128)S(1)}, s32[]{:T(128)}) while((s32[]{:T(128)}, f32[6,4]{1,0:T(8,128)S(1)}, f32[32,6,4]{1,2,0:T(4,128)S(1)}, f32[32,6,4]{2,1,0:T(8,128)S(1)}, s32[]{:T(128)}) %tuple.713), condition=%wide.region_27.28_spmd, body=%wide.region_26.27_spmd.sunk | while | flops 102 | bytes 5205 | solution.py:108
  206.5 6.7 %while.324 = (s32[]{:T(128)}, f32[6,4]{1,0:T(8,128)S(1)}, f32[32,6,4]{1,2,0:T(4,128)S(1)}, f32[32,6,4]{2,1,0:T(8,128)S(1)}, s32[]{:T(128)}, /*index=5*/s32[]{:T(128)}) while((s32[]{:T(128)}, f32[6,4]{1,0:T(8,128)S(1)}, f32[32,6,4]{1,2,0:T(4,128)S(1)}, f32[32,6,4]{2,1,0:T(8,128)S(1)}, s32[]{:T(128)}, /*index=5*/s32[]{:T(128)}) %tuple.741), condition=%wide.region_25.26_spmd, body=%wide.region_24.25_spmd.sunk | while | flops 103 | bytes 5225 | solution.py:113
  213.7 10.9 %all_to_all.84 = f32[128,32,4]{0,2,1:T(4,128)S(1)} all-to-all(f32[128,32,4]{0,2,1:T(4,128)S(1)} %bitcast.1267), channel_id=1, replica_groups=mesh['gx'=4,'gy'=32] {'gy'}, dimensions={1} | all-to-all | bytes 131072 | tf_op jit(solution)/shard_map/all_to_all | solution.py:217
  232.6 9.6 %while.340 = (s32[]{:T(128)}, f32[128]{0:T(128)S(1)}, f32[128,128]{1,0:T(8,128)S(1)}, f32[128,128]{1,0:T(8,128)S(1)}, f32[128,128]{1,0:T(8,128)S(1)}, /*index=5*/f32[128,128]{1,0:T(8,128)S(1)}, s32[]{:T(128)}, s32[]{:T(128)}) while((s32[]{:T(128)}, f32[128]{0:T(128)S(1)}, f32[128,128]{1,0:T(8,128)S(1)}, ...), condition=%wide.region_29.30_spmd.clone, body=%wide.region_28.29_spmd.clone.sunk | while | flops 515 | bytes 3687 | solution.py:51
  242.3 9.6 %while.341 = (s32[]{:T(128)}, f32[128]{0:T(128)S(1)}, f32[128,128]{1,0:T(8,128)S(1)}, f32[128,128]{1,0:T(8,128)S(1)}, f32[128,128]{1,0:T(8,128)S(1)}, /*index=5*/s32[]{:T(128)}, s32[]{:T(128)}, s32[]{:T(128)}) while((s32[]{:T(128)}, f32[128]{0:T(128)S(1)}, f32[128,128]{1,0:T(8,128)S(1)}, f32[128,128]{1,0:T(8,128)S(1)}, ...), condition=%wide.region_31.32_spmd.clone, body=%wide.region_30.31_spmd.clone.sunk | while | flops 388 | bytes 3187 | solution.py:58
  251.9 9.0 %all-gather.3 = f32[4,6,128]{2,1,0:T(8,128)S(1)} all-gather(f32[1,6,128]{2,1,0:T(8,128)S(1)} %bitcast.1282), channel_id=3, replica_groups=mesh['gx'=4,'gy'=32] {'gx'}, dimensions={0}, use_global_device_ids=true | all-gather | bytes 15360 | tf_op jit(solution)/shard_map/all_gather | solution.py:192
  263.4 4.0 %collective-permute-start.11 = (f32[1,128]{1,0:T(1,128)S(1)}, f32[1,128]{1,0:T(1,128)S(1)}, u32[]{:S(2)}, u32[]{:S(2)}) collective-permute-start(f32[1,128]{1,0:T(1,128)S(1)} %get-tuple-element.2075), channel_id=1, source_target_pairs={{0,32},{32,64},{64,96},{1,33},{33,65},{65,97},{2,34},{34,66},{66,9... | collective-permute-start | bytes 1544 | tf_op jit(solution)/shard_map/ppermute | solution.py:24
  269.6 11.6 %all-to-all-start.6 = ((f32[128,32,4]{0,2,1:T(4,128)}), f32[128,32,4]{0,2,1:T(4,128)S(1)}, u32[]{:S(2)}, u32[]{:S(2)}) async-start(f32[128,32,4]{0,2,1:T(4,128)} %bitcast.110), calls=%async_computation.6 | async-start | bytes 131072 | tf_op jit(solution)/shard_map/all_to_all | solution.py:209
  281.3 7.3 %all-to-all-done.6 = f32[128,32,4]{0,2,1:T(4,128)S(1)} async-done(((f32[128,32,4]{0,2,1:T(4,128)}), f32[128,32,4]{0,2,1:T(4,128)S(1)}, u32[]{:S(2)}, u32[]{:S(2)}) %all-to-all-start.6) | async-done | bytes 65568 | tf_op jit(solution)/shard_map/all_to_all | solution.py:209
  288.7 9.6 %while.342 = (s32[]{:T(128)}, f32[128]{0:T(128)S(1)}, f32[128,128]{1,0:T(8,128)S(1)}, f32[128,128]{1,0:T(8,128)S(1)}, f32[128,128]{1,0:T(8,128)S(1)}, /*index=5*/f32[128,128]{1,0:T(8,128)S(1)}, s32[]{:T(128)}, s32[]{:T(128)}) while((s32[]{:T(128)}, f32[128]{0:T(128)S(1)}, f32[128,128]{1,0:T(8,128)S(1)}, ...), condition=%wide.region_37.38_spmd.clone, body=%wide.region_36.37_spmd.clone.sunk | while | flops 515 | bytes 3687 | solution.py:51
  298.3 9.6 %while.343 = (s32[]{:T(128)}, f32[128]{0:T(128)S(1)}, f32[128,128]{1,0:T(8,128)S(1)}, f32[128,128]{1,0:T(8,128)S(1)}, f32[128,128]{1,0:T(8,128)S(1)}, /*index=5*/s32[]{:T(128)}, s32[]{:T(128)}, s32[]{:T(128)}) while((s32[]{:T(128)}, f32[128]{0:T(128)S(1)}, f32[128,128]{1,0:T(8,128)S(1)}, f32[128,128]{1,0:T(8,128)S(1)}, ...), condition=%wide.region_39.40_spmd.clone, body=%wide.region_38.39_spmd.clone.sunk | while | flops 388 | bytes 3187 | solution.py:58
  308.8 6.7 %while.329 = (s32[]{:T(128)}, f32[6,4]{1,0:T(8,128)S(1)}, f32[32,6,4]{1,2,0:T(4,128)S(1)}, f32[32,6,4]{2,1,0:T(8,128)S(1)}, s32[]{:T(128)}) while((s32[]{:T(128)}, f32[6,4]{1,0:T(8,128)S(1)}, f32[32,6,4]{1,2,0:T(4,128)S(1)}, f32[32,6,4]{2,1,0:T(8,128)S(1)}, s32[]{:T(128)}) %tuple.737), condition=%wide.region_43.44_spmd, body=%wide.region_42.43_spmd.sunk | while | flops 102 | bytes 5205 | solution.py:108
  316.0 6.7 %while.328 = (s32[]{:T(128)}, f32[6,4]{1,0:T(8,128)S(1)}, f32[32,6,4]{1,2,0:T(4,128)S(1)}, f32[32,6,4]{2,1,0:T(8,128)S(1)}, s32[]{:T(128)}, /*index=5*/s32[]{:T(128)}) while((s32[]{:T(128)}, f32[6,4]{1,0:T(8,128)S(1)}, f32[32,6,4]{1,2,0:T(4,128)S(1)}, f32[32,6,4]{2,1,0:T(8,128)S(1)}, s32[]{:T(128)}, /*index=5*/s32[]{:T(128)}) %tuple.740), condition=%wide.region_41.42_spmd, body=%wide.region_40.41_spmd.sunk | while | flops 103 | bytes 5225 | solution.py:113
  323.2 10.9 %all_to_all.85 = f32[128,32,4]{0,2,1:T(4,128)S(1)} all-to-all(f32[128,32,4]{0,2,1:T(4,128)S(1)} %bitcast.1266), channel_id=1, replica_groups=mesh['gx'=4,'gy'=32] {'gy'}, dimensions={1} | all-to-all | bytes 131072 | tf_op jit(solution)/shard_map/all_to_all | solution.py:217
  (5010 shorter events, 174.0 us)
Async XLA Ops:
  0.7 13.6 %collective-permute-start = (f32[1,128]{1,0:T(1,128)S(1)}, f32[1,128]{1,0:T(1,128)S(1)}, u32[]{:S(2)}, u32[]{:S(2)}) collective-permute-start(f32[1,128]{1,0:T(1,128)S(1)} %get-tuple-element.2088), channel_id=1, source_target_pairs={{0,32},{32,64},{64,96},{1,33},{33,65},{65,97},{2,34},{34,66},{66,9... | collective-permute-start | bytes 1544 | tf_op jit(solution)/shard_map/ppermute | solution.py:24
  4.7 9.7 %collective-permute-start.1 = (f32[1,128]{1,0:T(1,128)S(1)}, f32[1,128]{1,0:T(1,128)S(1)}, u32[]{:S(2)}, u32[]{:S(2)}) collective-permute-start(f32[1,128]{1,0:T(1,128)S(1)} %get-tuple-element.2087), channel_id=1, source_target_pairs={{32,0},{64,32},{96,64},{33,1},{65,33},{97,65},{34,2},{66,34},{98,6... | collective-permute-start | bytes 1544 | tf_op jit(solution)/shard_map/ppermute | solution.py:25
  7.0 28.6 %collective-permute-start.4 = (f32[128,1]{1,0:T(8,128)S(1)}, f32[128,1]{1,0:T(8,128)S(1)}, u32[]{:S(2)}, u32[]{:S(2)}) collective-permute-start(f32[128,1]{1,0:T(8,128)S(1)} %get-tuple-element.2089), channel_id=1, source_target_pairs={{1,0},{2,1},{3,2},{4,3},{5,4},{6,5},{7,6},{8,7},{9,8},{10,9},{11,1... | collective-permute-start | bytes 1544 | tf_op jit(solution)/shard_map/ppermute | solution.py:25
  9.8 25.8 %collective-permute-start.5 = (f32[128,1]{1,0:T(8,128)S(1)}, f32[128,1]{1,0:T(8,128)S(1)}, u32[]{:S(2)}, u32[]{:S(2)}) collective-permute-start(f32[128,1]{1,0:T(8,128)S(1)} %get-tuple-element.2090), channel_id=1, source_target_pairs={{0,1},{1,2},{2,3},{3,4},{4,5},{5,6},{6,7},{7,8},{8,9},{9,10},{10,1... | collective-permute-start | bytes 1544 | tf_op jit(solution)/shard_map/ppermute | solution.py:24
  13.1 0.7 copy-start.4
  14.0 0.8 copy-start
  15.0 20.5 %collective-permute-start.2 = (f32[130,1]{1,0:T(8,128)S(1)}, f32[130,1]{1,0:T(8,128)S(1)}, u32[]{:S(2)}, u32[]{:S(2)}) collective-permute-start(f32[130,1]{1,0:T(8,128)S(1)} %get-tuple-element.2072), channel_id=1, source_target_pairs={{0,1},{1,2},{2,3},{3,4},{4,5},{5,6},{6,7},{7,8},{8,9},{9,10},{10,1... | collective-permute-start | bytes 1568 | tf_op jit(solution)/shard_map/ppermute | solution.py:24
  17.4 18.1 %collective-permute-start.3 = (f32[130,1]{1,0:T(8,128)S(1)}, f32[130,1]{1,0:T(8,128)S(1)}, u32[]{:S(2)}, u32[]{:S(2)}) collective-permute-start(f32[130,1]{1,0:T(8,128)S(1)} %get-tuple-element.2073), channel_id=1, source_target_pairs={{1,0},{2,1},{3,2},{4,3},{5,4},{6,5},{7,6},{8,7},{9,8},{10,9},{11,1... | collective-permute-start | bytes 1568 | tf_op jit(solution)/shard_map/ppermute | solution.py:25
  35.4 0.8 copy-start.1
  35.4 0.9 copy-start.2
  38.0 29.0 %all-to-all-start.2 = ((f32[128,32,4]{0,2,1:T(4,128)}), f32[128,32,4]{0,2,1:T(4,128)S(1)}, u32[]{:S(2)}, u32[]{:S(2)}) async-start(f32[128,32,4]{0,2,1:T(4,128)} %bitcast.79), calls=%async_computation.2 | async-start | bytes 131072 | tf_op jit(solution)/shard_map/all_to_all | solution.py:171
  67.0 14.7 %all-to-all-start.1 = ((f32[128,32,4]{0,2,1:T(4,128)}), f32[128,32,4]{0,2,1:T(4,128)S(1)}, u32[]{:S(2)}, u32[]{:S(2)}) async-start(f32[128,32,4]{0,2,1:T(4,128)} %bitcast.76), calls=%async_computation.1 | async-start | bytes 131072 | tf_op jit(solution)/shard_map/all_to_all | solution.py:170
  81.7 31.2 %all-to-all-start.3 = ((f32[128,32,4]{0,2,1:T(4,128)}), f32[128,32,4]{0,2,1:T(4,128)S(1)}, u32[]{:S(2)}, u32[]{:S(2)}) async-start(f32[128,32,4]{0,2,1:T(4,128)} %bitcast.82), calls=%async_computation.3 | async-start | bytes 131072 | tf_op jit(solution)/shard_map/all_to_all | solution.py:168
  111.2 0.7 copy-start.3
  112.9 17.7 %all-to-all-start.4 = ((f32[128,32,4]{0,2,1:T(4,128)}), f32[128,32,4]{0,2,1:T(4,128)S(1)}, u32[]{:S(2)}, u32[]{:S(2)}) async-start(f32[128,32,4]{0,2,1:T(4,128)} %bitcast.84), calls=%async_computation.4 | async-start | bytes 131072 | tf_op jit(solution)/shard_map/all_to_all | solution.py:169
  145.5 20.1 %collective-permute-start.6 = (f32[1,128]{1,0:T(1,128)S(1)}, f32[1,128]{1,0:T(1,128)S(1)}, u32[]{:S(2)}, u32[]{:S(2)}) collective-permute-start(f32[1,128]{1,0:T(1,128)S(1)} %get-tuple-element.2083), channel_id=1, source_target_pairs={{32,0},{64,32},{96,64},{33,1},{65,33},{97,65},{34,2},{66,34},{98,6... | collective-permute-start | bytes 1544 | tf_op jit(solution)/shard_map/ppermute | solution.py:25
  146.8 18.8 %collective-permute-start.7 = (f32[1,128]{1,0:T(1,128)S(1)}, f32[1,128]{1,0:T(1,128)S(1)}, u32[]{:S(2)}, u32[]{:S(2)}) collective-permute-start(f32[1,128]{1,0:T(1,128)S(1)} %get-tuple-element.2084), channel_id=1, source_target_pairs={{0,32},{32,64},{64,96},{1,33},{33,65},{65,97},{2,34},{34,66},{66,9... | collective-permute-start | bytes 1544 | tf_op jit(solution)/shard_map/ppermute | solution.py:24
  167.2 11.9 %all-to-all-start = ((f32[128,32,4]{0,2,1:T(4,128)}), f32[128,32,4]{0,2,1:T(4,128)S(1)}, u32[]{:S(2)}, u32[]{:S(2)}) async-start(f32[128,32,4]{0,2,1:T(4,128)} %bitcast.73), calls=%async_computation | async-start | bytes 131072 | tf_op jit(solution)/shard_map/all_to_all | solution.py:209
  224.7 5.6 %collective-permute-start.8 = (f32[128,1]{1,0:T(8,128)S(1)}, f32[128,1]{1,0:T(8,128)S(1)}, u32[]{:S(2)}, u32[]{:S(2)}) collective-permute-start(f32[128,1]{1,0:T(8,128)S(1)} %get-tuple-element.2078), channel_id=1, source_target_pairs={{1,0},{2,1},{3,2},{4,3},{5,4},{6,5},{7,6},{8,7},{9,8},{10,9},{11,1... | collective-permute-start | bytes 1544 | tf_op jit(solution)/shard_map/ppermute | solution.py:25
  227.0 4.6 %collective-permute-start.9 = (f32[128,1]{1,0:T(8,128)S(1)}, f32[128,1]{1,0:T(8,128)S(1)}, u32[]{:S(2)}, u32[]{:S(2)}) collective-permute-start(f32[128,1]{1,0:T(8,128)S(1)} %get-tuple-element.2079), channel_id=1, source_target_pairs={{0,1},{1,2},{2,3},{3,4},{4,5},{5,6},{6,7},{7,8},{8,9},{9,10},{10,1... | collective-permute-start | bytes 1544 | tf_op jit(solution)/shard_map/ppermute | solution.py:24
  262.1 5.3 %collective-permute-start.10 = (f32[1,128]{1,0:T(1,128)S(1)}, f32[1,128]{1,0:T(1,128)S(1)}, u32[]{:S(2)}, u32[]{:S(2)}) collective-permute-start(f32[1,128]{1,0:T(1,128)S(1)} %get-tuple-element.2074), channel_id=1, source_target_pairs={{32,0},{64,32},{96,64},{33,1},{65,33},{97,65},{34,2},{66,34},{98,6... | collective-permute-start | bytes 1544 | tf_op jit(solution)/shard_map/ppermute | solution.py:25
  263.4 4.7 %collective-permute-start.11 = (f32[1,128]{1,0:T(1,128)S(1)}, f32[1,128]{1,0:T(1,128)S(1)}, u32[]{:S(2)}, u32[]{:S(2)}) collective-permute-start(f32[1,128]{1,0:T(1,128)S(1)} %get-tuple-element.2075), channel_id=1, source_target_pairs={{0,32},{32,64},{64,96},{1,33},{33,65},{65,97},{2,34},{34,66},{66,9... | collective-permute-start | bytes 1544 | tf_op jit(solution)/shard_map/ppermute | solution.py:24
  269.6 19.0 %all-to-all-start.6 = ((f32[128,32,4]{0,2,1:T(4,128)}), f32[128,32,4]{0,2,1:T(4,128)S(1)}, u32[]{:S(2)}, u32[]{:S(2)}) async-start(f32[128,32,4]{0,2,1:T(4,128)} %bitcast.110), calls=%async_computation.6 | async-start | bytes 131072 | tf_op jit(solution)/shard_map/all_to_all | solution.py:209
where the time goes:
time: 336 us; the launch traced here: 335 us
  local copies, waits for them, and re-layouts  92 us (27%)
  starting transfers between devices  79 us (24%)
  other arithmetic  46.9 us (14%)
  loops' own time  44.3 us (13%)
  blocking collectives  41.1 us (12%)
  waiting for transfers between devices  30.3 us (9%)
    dynamic_update_slice x1536, local copies, waits for them, and re-layouts, factor(): lax.scan(advance, jnp.zeros_like(main_diag[0]), (sub_diag, main_diag, sup...  57.8 us
    all_to_all x2, blocking collectives, local(): lax.all_to_all(column_drop, 'gy', split_axis=1, concat_axis=1, tiled=True)  21.7 us
    ppermute x6, starting transfers between devices, with_halo(): before = lax.ppermute(last, axis, up)  20.7 us
    all_gather x2, blocking collectives, local(): gathered = lax.all_gather(solve_own_rel[None], 'gx', axis=0, tiled=True)  19.3 us
    another operation x6, loops' own time, substitute(): lax.scan(backward, jnp.zeros_like(source[0]), (ratios, partial_sol), reve...  16.7 us
    another operation x6, loops' own time, substitute(): lax.scan(forward, jnp.zeros_like(source[0]), (sub_diag, pivots, source))  16.7 us
    all_to_all x2, starting transfers between devices, local(): lax.all_to_all(source.T, 'gy', split_axis=1, concat_axis=1, tiled=True)  16.1 us
    all_to_all x2, waiting for transfers between devices, local(): lax.all_to_all(source.T, 'gy', split_axis=1, concat_axis=1, tiled=True)  14 us

commit v1 on v0

v1 whole, which is shorter than its diff:
```python
import jax
import jax.numpy as jnp
from jax import lax
from jax.experimental import pallas as pl
from jax.experimental.pallas import tpu as pltpu
from jax.sharding import PartitionSpec as P

PITCH = 32
xward_admittance = 1.0
yward_admittance = 0.5
warmth_scaling = 0.004
surrounding_warmth = 25.0
cushion_pieces = 1.0

SUB = 8
LANES = 128
ROWS = 128
DEPTH = ROWS // SUB
COUNT_X = 4
COUNT_Y = 32
Y_DEPTH = COUNT_Y // SUB

INNER = (
    [(m, m - 1, m + 1) for m in range(1, DEPTH - 2, 2)]
    + [(2, 0, 4), (6, 4, 8), (10, 8, 12), (14, 12, 15)]
    + [(4, 0, 8), (12, 8, 15), (8, 0, 15)]
)
SPANS = (1, 2, 4)
LOCAL_COEFS = 3 * (len(INNER) + 1 + len(SPANS))

def path_order(nodes):
    order = []
    while len(nodes) > 1:
        for at in range(1, len(nodes), 2):
            right = nodes[at + 1] if at + 1 < len(nodes) else None
            order.append((nodes[at], nodes[at - 1], right))
        nodes = nodes[::2]
    return order + [(nodes[0], None, None)]


X_ORDER = path_order(list(range(2 * COUNT_X)))
X_COEFS = 3 * len(X_ORDER)
Y_ORDER = [(1, 0, 2), (3, 2, 4), (5, 4, 6), (7, 6, 8), (2, 0, 4), (6, 4, 8), (4, 0, 8)]
Y_COEFS = 3 * (len(Y_ORDER) + len(SPANS)) + 1


def wire(admittance, warm_a, warm_b):
    return admittance / (1.0 + warmth_scaling * (0.5 * (warm_a + warm_b) - surrounding_warmth))


def sublanes():
    return lax.broadcasted_iota(jnp.int32, (SUB, LANES), 0)


def roll(x, by):
    return pltpu.roll(x, by % SUB, 0)


def spread(row):
    return jnp.broadcast_to(row, (SUB, LANES))


def load_lines(ref):
    return [ref[pl.ds(r, SUB, stride=DEPTH), :] for r in range(DEPTH)]


def store_lines(ref, values):
    for r in range(DEPTH):
        ref[pl.ds(r, SUB, stride=DEPTH), :] = values[r]


def load_regs(ref, count=DEPTH):
    return [ref[pl.ds(SUB * r, SUB), :] for r in range(count)]


def store_regs(ref, values):
    for r, value in enumerate(values):
        ref[pl.ds(SUB * r, SUB), :] = value


def coef(ref, k):
    return [ref[pl.ds(SUB * (3 * k + n), SUB), :] for n in range(3)]


def put_coef(ref, k, values):
    for n, value in enumerate(values):
        ref[pl.ds(SUB * (3 * k + n), SUB), :] = value


def factor_local(ref, ground, edges, across):
    sub = sublanes()
    edges = dict(edges)
    for k, (m, left, right) in enumerate(INNER):
        to_left, to_right = edges[(left, m)], edges[(m, right)]
        inverse = 1.0 / (to_left + to_right + ground[m])
        by_left, by_right = to_left * inverse, to_right * inverse
        ground[left] = ground[left] + by_left * ground[m]
        ground[right] = ground[right] + by_right * ground[m]
        edges[(left, right)] = to_left * by_right
        put_coef(ref, k, (inverse, by_left, by_right))
    own, first, last = edges[(0, DEPTH - 1)], ground[0], ground[DEPTH - 1]
    inside = sub < SUB - 1
    inverse = jnp.where(inside, 1.0 / (own + across + last), 0.0)
    by_left, by_right = own * inverse, across * inverse
    put_coef(ref, len(INNER), (inverse, by_left, by_right))
    edge = jnp.where(inside, own * by_right, own)
    end = roll(last, 1)
    first = first + by_left * last + roll(by_right * last, 1)
    for n, span in enumerate(SPANS):
        chosen = sub % (2 * span) == span
        to_left = roll(edge, span)
        inverse = jnp.where(chosen, 1.0 / (to_left + edge + first), 0.0)
        by_left, by_right = to_left * inverse, edge * inverse
        put_coef(ref, len(INNER) + 1 + n, (inverse, by_left, by_right))
        passed = roll(by_right * first, span)
        end = end + passed
        first = first + roll(by_left * first, -span) + jnp.where(sub == 0, 0.0, passed)
        edge = roll(to_left * by_right, -span)
    return edge[0:1], first[0:1], end[0:1]


def forward_local(ref, f):
    sub = sublanes()
    for k, (m, left, right) in enumerate(INNER):
        _, by_left, by_right = coef(ref, k)
        f[left] = f[left] + by_left * f[m]
        f[right] = f[right] + by_right * f[m]
    first, last = f[0], f[DEPTH - 1]
    _, by_left, by_right = coef(ref, len(INNER))
    end = roll(last, 1)
    first = first + by_left * last + roll(by_right * last, 1)
    for n, span in enumerate(SPANS):
        _, by_left, by_right = coef(ref, len(INNER) + 1 + n)
        passed = roll(by_right * first, span)
        end = end + passed
        first = first + roll(by_left * first, -span) + jnp.where(sub == 0, 0.0, passed)
    f[0] = first
    return first[0:1], end[0:1]


def backward_local(ref, f, first, end):
    sub = sublanes()
    x = jnp.where(sub == 0, first, 0.0)
    for n in range(len(SPANS) - 1, -1, -1):
        span = SPANS[n]
        inverse, by_left, by_right = coef(ref, len(INNER) + 1 + n)
        beyond = roll(jnp.where(sub == 0, end, x), -span)
        found = inverse * f[0] + by_left * roll(x, span) + by_right * beyond
        x = jnp.where(sub % (2 * span) == span, found, x)
    inverse, by_left, by_right = coef(ref, len(INNER))
    found = inverse * f[DEPTH - 1] + by_left * x + by_right * roll(x, -1)
    out = [None] * DEPTH
    out[0] = x
    out[DEPTH - 1] = jnp.where(sub == SUB - 1, end, found)
    for k in range(len(INNER) - 1, -1, -1):
        m, left, right = INNER[k]
        inverse, by_left, by_right = coef(ref, k)
        out[m] = inverse * f[m] + by_left * out[left] + by_right * out[right]
    return out


def put_rows(ref, rows):
    for n, row in enumerate(rows):
        ref[n : n + 1, :] = row


def gather_x(joined, own, others):
    place = lax.axis_index("gx")
    count = own.shape[0]
    joined[pl.ds(pl.multiple_of(place * SUB, SUB), count), :] = own[...]
    for n, other in enumerate(others):
        source = lax.rem(place + COUNT_X - (n + 1), COUNT_X)
        joined[pl.ds(pl.multiple_of(source * SUB, SUB), count), :] = other[...]


def factor_x(ref, joined):
    def row(p, q):
        return spread(joined[SUB * p + q : SUB * p + q + 1, :])

    ground, edges = {}, {}
    for p in range(COUNT_X):
        ground[2 * p], ground[2 * p + 1] = row(p, 2), row(p, 3)
        edges[(2 * p, 2 * p + 1)] = row(p, 4)
        if p + 1 < COUNT_X:
            edges[(2 * p + 1, 2 * p + 2)] = wire(xward_admittance, row(p, 6), row(p + 1, 5))
    for k, (m, left, right) in enumerate(X_ORDER):
        total = ground[m]
        if left is not None:
            total = total + edges[(left, m)]
        if right is not None:
            total = total + edges[(m, right)]
        inverse = 1.0 / total
        by_left = edges[(left, m)] * inverse if left is not None else inverse
        by_right = edges[(m, right)] * inverse if right is not None else inverse
        if left is not None:
            ground[left] = ground[left] + by_left * ground[m]
        if right is not None:
            ground[right] = ground[right] + by_right * ground[m]
        if left is not None and right is not None:
            edges[(left, right)] = edges[(left, m)] * by_right
        put_coef(ref, k, (inverse, by_left, by_right))


def solve_x(ref, joined):
    f = [
        spread(joined[SUB * (n // 2) + n % 2 : SUB * (n // 2) + n % 2 + 1, :])
        for n in range(2 * COUNT_X)
    ]
    for k, (m, left, right) in enumerate(X_ORDER):
        _, by_left, by_right = coef(ref, k)
        if left is not None:
            f[left] = f[left] + by_left * f[m]
        if right is not None:
            f[right] = f[right] + by_right * f[m]
    x = [None] * len(f)
    for k in range(len(X_ORDER) - 1, -1, -1):
        m, left, right = X_ORDER[k]
        inverse, by_left, by_right = coef(ref, k)
        x[m] = inverse * f[m]
        if left is not None:
            x[m] = x[m] + by_left * x[left]
        if right is not None:
            x[m] = x[m] + by_right * x[right]
    place = lax.axis_index("gx")
    first, end = x[0], x[1]
    for p in range(1, COUNT_X):
        first = jnp.where(place == p, x[2 * p], first)
        end = jnp.where(place == p, x[2 * p + 1], end)
    return first, end


def factor_y(ref, joined):
    sub = sublanes()

    def part(r, q):
        return joined[pl.ds(SUB * r + q, SUB, stride=SUB * Y_DEPTH), :]

    ground, edges = {}, {}
    for r in range(Y_DEPTH):
        ground[2 * r], ground[2 * r + 1] = part(r, 2), part(r, 3)
        edges[(2 * r, 2 * r + 1)], edges[(2 * r + 1, 2 * r + 2)] = part(r, 4), part(r, 5)
    last = 2 * Y_DEPTH
    for k, (m, left, right) in enumerate(Y_ORDER):
        to_left, to_right = edges[(left, m)], edges[(m, right)]
        inverse = 1.0 / (to_left + to_right + ground[m])
        by_left, by_right = to_left * inverse, to_right * inverse
        put_coef(ref, k, (inverse, by_left, by_right))
        ground[left] = ground[left] + by_left * ground[m]
        passed = by_right * ground[m]
        if right == last:
            ground[0] = ground[0] + roll(passed, 1)
        else:
            ground[right] = ground[right] + passed
        edges[(left, right)] = to_left * by_right
    edge, first = edges[(0, last)], ground[0]
    for n, span in enumerate(SPANS):
        chosen = sub % (2 * span) == span
        to_left = roll(edge, span)
        inverse = jnp.where(chosen, 1.0 / (to_left + edge + first), 0.0)
        by_left, by_right = to_left * inverse, edge * inverse
        put_coef(ref, len(Y_ORDER) + n, (inverse, by_left, by_right))
        first = first + roll(by_left * first, -span) + roll(by_right * first, span)
        edge = roll(to_left * by_right, -span)
    ref[pl.ds(SUB * (Y_COEFS - 1), SUB), :] = jnp.where(sub == 0, 1.0 / first, 0.0)


def solve_y(ref, joined, stride, found):
    sub = sublanes()
    last = 2 * Y_DEPTH
    f = [
        joined[pl.ds(stride * (n // 2) + n % 2, SUB, stride=stride * Y_DEPTH), :]
        for n in range(last)
    ]
    for k, (m, left, right) in enumerate(Y_ORDER):
        _, by_left, by_right = coef(ref, k)
        f[left] = f[left] + by_left * f[m]
        if right == last:
            f[0] = f[0] + roll(by_right * f[m], 1)
        else:
            f[right] = f[right] + by_right * f[m]
    first = f[0]
    for n, span in enumerate(SPANS):
        _, by_left, by_right = coef(ref, len(Y_ORDER) + n)
        first = first + roll(by_left * first, -span) + roll(by_right * first, span)
    x0 = ref[pl.ds(SUB * (Y_COEFS - 1), SUB), :] * first
    for n in range(len(SPANS) - 1, -1, -1):
        span = SPANS[n]
        inverse, by_left, by_right = coef(ref, len(Y_ORDER) + n)
        value = inverse * first + by_left * roll(x0, span) + by_right * roll(x0, -span)
        x0 = jnp.where(sub % (2 * span) == span, value, x0)
    x = [x0] + [None] * (last - 1) + [roll(x0, -1)]
    for k in range(len(Y_ORDER) - 1, -1, -1):
        m, left, right = Y_ORDER[k]
        inverse, by_left, by_right = coef(ref, k)
        x[m] = inverse * f[m] + by_left * x[left] + by_right * x[right]
    store_regs(found, x[:last])
    place = lax.axis_index("gy")
    at = lax.rem(place, Y_DEPTH) * (2 * SUB) + lax.div(place, Y_DEPTH)
    return spread(found[pl.ds(at, 1), :]), spread(found[pl.ds(at + SUB, 1), :])


def prepare(v, warm, v_t, warm_t, inside, outside):
    v_t[...] = v[...].T
    warm_t[...] = warm[...].T
    odd = lax.rem(lax.axis_index("gy"), 2) == 1
    for n, ref in enumerate((v_t, warm_t)):
        low, high = ref[0:1, :], ref[ROWS - 1 : ROWS, :]
        inside[n : n + 1, :] = jnp.where(odd, low, high)
        outside[n : n + 1, :] = jnp.where(odd, high, low)


def pads(flags, transposed):
    sub = sublanes()
    lane = lax.broadcasted_iota(jnp.int32, (SUB, LANES), 1)
    out = jnp.zeros((SUB, LANES), jnp.float32)
    for a in range(ROWS // PITCH):
        for b in range(LANES // PITCH):
            flag = flags[b, a] if transposed else flags[a, b]
            here = (sub == a * (PITCH // DEPTH)) & (lane == b * PITCH)
            out = jnp.where(here & (flag == 1), cushion_pieces, out)
    return out


def coefficients(cap, warm, warm_t, flags, x_ref, y_ref, cap_t, x_rows, y_rows, y_edges, y_pad):
    cap_t[...] = cap[...].T
    for transposed, caps, warms, ref, rows in (
        (False, cap, warm, x_ref, x_rows),
        (True, cap_t, warm_t, y_ref, y_rows),
    ):
        admittance = yward_admittance if transposed else xward_admittance
        temps = load_lines(warms)
        edges = {(r, r + 1): wire(admittance, temps[r], temps[r + 1]) for r in range(DEPTH - 1)}
        across = wire(admittance, temps[DEPTH - 1], roll(temps[0], -1))
        pad = pads(flags, transposed)
        if transposed:
            store_regs(y_edges, [edges[(r, r + 1)] for r in range(DEPTH - 1)] + [across])
            y_pad[...] = pad
        ground = load_lines(caps)
        ground[0] = ground[0] + pad
        own, first, end = factor_local(ref, ground, edges, across)
        rows[...] = jnp.zeros((SUB, LANES), jnp.float32)
        rows[2:3, :] = first
        rows[3:4, :] = end
        rows[4:5, :] = own
        if not transposed:
            rows[5:6, :] = warms[0:1, :]
            rows[6:7, :] = warms[ROWS - 1 : ROWS, :]


def begin(
    v_t, warm_t, cap_t, load, inside, outside, y_edges, y_pad, y_rows, x_ref, x_rows,
    s_out, f_out, sent, y_rows_out, flat,
):
    sub = sublanes()
    place = lax.axis_index("gy")
    odd = lax.rem(place, 2) == 1
    low_v = jnp.where(odd, inside[0:1, :], outside[0:1, :])
    low_warm = jnp.where(odd, inside[1:2, :], outside[1:2, :])
    high_v = jnp.where(odd, outside[0:1, :], inside[0:1, :])
    high_warm = jnp.where(odd, outside[1:2, :], inside[1:2, :])
    low_edge = wire(yward_admittance, low_warm, warm_t[0:1, :])
    high_edge = wire(yward_admittance, warm_t[ROWS - 1 : ROWS, :], high_warm)
    low_edge = jnp.where(place > 0, low_edge, 0.0)
    high_edge = jnp.where(place < COUNT_Y - 1, high_edge, 0.0)
    y_rows_out[...] = y_rows[...]
    y_rows_out[5:6, :] = high_edge
    v = load_lines(v_t)
    cap = load_lines(cap_t)
    edges = load_regs(y_edges)
    before = jnp.where(sub == 0, spread(low_v), roll(v[DEPTH - 1], 1))
    before_edge = jnp.where(sub == 0, spread(low_edge), roll(edges[DEPTH - 1], 1))
    after = jnp.where(sub == SUB - 1, spread(high_v), roll(v[0], -1))
    edges[DEPTH - 1] = jnp.where(sub == SUB - 1, spread(high_edge), edges[DEPTH - 1])
    flow = before_edge * (before - v[0])
    out = []
    for r in range(DEPTH):
        onward = edges[r] * ((v[r + 1] if r + 1 < DEPTH else after) - v[r])
        own = cap[r] * v[r]
        if r == 0:
            own = own - y_pad[...] * v[r]
        out.append(own + (flow + onward))
        flow = -onward
    store_lines(flat, out)
    flat[...] = flat[...].T + load[0]
    s = load_lines(flat)
    store_regs(s_out, s)
    first, end = forward_local(x_ref, s)
    store_regs(f_out, s)
    sent[...] = x_rows[...]
    sent[0:1, :] = first
    sent[1:2, :] = end


def across_x(
    own, one, two, three, cap, load, step, s_in, f_in, x_ref, y_ref, x_join, s_out, f_out, joined, flat
):
    first, end = solve_x(x_join, joined)
    half = backward_local(x_ref, load_regs(f_in), first, end)
    caps, source = load_lines(cap), load_regs(s_in)
    loads = load_lines(load.at[step])
    store_lines(
        flat, [2.0 * caps[r] * half[r] - source[r] + loads[r] for r in range(DEPTH)]
    )
    flat[...] = flat[...].T
    s = load_lines(flat)
    if s_out is not None:
        store_regs(s_out, s)
    ends = forward_local(y_ref, s)
    store_regs(f_out, s)
    return ends


def first_x(
    own, one, two, three, cap, load, s_in, f_in, x_ref, y_ref, y_rows,
    x_join, s_out, f_out, sent, joined, flat,
):
    gather_x(joined, own, (one, two, three))
    factor_x(x_join, joined)
    first, end = across_x(
        own, one, two, three, cap, load, 0, s_in, f_in, x_ref, y_ref, x_join, s_out, f_out, joined, flat
    )
    sent[...] = y_rows[...]
    sent[0:1, :] = first
    sent[1:2, :] = end


def second_x(
    own, one, two, three, cap, load, s_in, f_in, x_ref, y_ref, x_join, f_out, sent, joined, flat
):
    gather_x(joined, own, (one, two, three))
    first, end = across_x(
        own, one, two, three, cap, load, 1, s_in, f_in, x_ref, y_ref, x_join, None, f_out, joined, flat
    )
    sent[0:1, :] = first
    sent[1:2, :] = end


def first_y(
    joined, cap_t, load, s_in, f_in, y_ref, x_ref, y_join, s_out, f_out, sent, found, flat
):
    factor_y(y_join, joined)
    first, end = solve_y(y_join, joined, SUB, found)
    drop = backward_local(y_ref, load_regs(f_in), first, end)
    caps, source = load_lines(cap_t), load_regs(s_in)
    store_lines(flat, [2.0 * caps[r] * drop[r] - source[r] for r in range(DEPTH)])
    flat[...] = flat[...].T + load[1]
    s = load_lines(flat)
    store_regs(s_out, s)
    first, end = forward_local(x_ref, s)
    store_regs(f_out, s)
    sent[0:1, :] = first
    sent[1:2, :] = end


def second_y(joined, f_in, y_ref, y_join, out, found, flat):
    first, end = solve_y(y_join, joined, 2, found)
    store_lines(flat, backward_local(y_ref, load_regs(f_in), first, end))
    out[...] = flat[...].T


def call(body, shapes, args, scratch=(), scalars=()):
    specs = [
        pl.BlockSpec(memory_space=pltpu.SMEM if n in scalars else pltpu.VMEM)
        for n in range(len(args))
    ]
    return pl.pallas_call(
        body,
        out_shape=[jax.ShapeDtypeStruct((rows, LANES), jnp.float32) for rows in shapes],
        in_specs=specs,
        out_specs=[pl.BlockSpec(memory_space=pltpu.VMEM)] * len(shapes),
        scratch_shapes=[pltpu.VMEM((rows, LANES), jnp.float32) for rows in scratch],
        name=body.__name__,
    )(*args)


def share_x(sent):
    return [
        lax.ppermute(sent, "gx", [(i, (i + by) % COUNT_X) for i in range(COUNT_X)])
        for by in range(1, COUNT_X)
    ]


def share_y(sent):
    rows = sent.shape[0]
    copies = jnp.broadcast_to(sent[None], (COUNT_Y, rows, LANES))
    return lax.all_to_all(copies, "gy", split_axis=0, concat_axis=0, tiled=True).reshape(
        COUNT_Y * rows, LANES
    )


def local(starting_sag, warmth_celsius_field, junction_charge_store, load_amperes, source_patch_bits):
    v, warm, cap, load = starting_sag, warmth_celsius_field, junction_charge_store, load_amperes
    v_t, warm_t, inside, outside = call(prepare, (ROWS, ROWS, 2, 2), (v, warm))
    inside = lax.ppermute(inside, "gy", [(i, i ^ 1) for i in range(COUNT_Y)])
    pairs = [(i, (i + 1) % COUNT_Y if i % 2 else (i - 1) % COUNT_Y) for i in range(COUNT_Y)]
    outside = lax.ppermute(outside, "gy", pairs)
    coefs = SUB * LOCAL_COEFS
    x_ref, y_ref, cap_t, x_rows, y_rows, y_edges, y_pad = call(
        coefficients,
        (coefs, coefs, ROWS, SUB, SUB, ROWS, SUB),
        (cap, warm, warm_t, source_patch_bits),
        scalars=(3,),
    )
    s, f, sent, y_rows = call(
        begin,
        (ROWS, ROWS, SUB, SUB),
        (v_t, warm_t, cap_t, load, inside, outside, y_edges, y_pad, y_rows, x_ref, x_rows),
        scratch=(ROWS,),
    )
    joined = COUNT_X * SUB
    x_join, s, f, sent = call(
        first_x,
        (SUB * X_COEFS, ROWS, ROWS, SUB),
        (sent, *share_x(sent), cap, load, s, f, x_ref, y_ref, y_rows),
        scratch=(joined, ROWS),
    )
    y_join, s, f, sent = call(
        first_y,
        (SUB * Y_COEFS, ROWS, ROWS, 2),
        (share_y(sent), cap_t, load, s, f, y_ref, x_ref),
        scratch=(2 * Y_DEPTH * SUB, ROWS),
    )
    f, sent = call(
        second_x,
        (ROWS, 2),
        (sent, *share_x(sent), cap, load, s, f, x_ref, y_ref, x_join),
        scratch=(joined, ROWS),
    )
    (drop,) = call(
        second_y,
        (ROWS,),
        (share_y(sent), f, y_ref, y_join),
        scratch=(2 * Y_DEPTH * SUB, ROWS),
    )
    return drop


def solution(mesh):
    return jax.shard_map(
        local,
        mesh=mesh,
        in_specs=(P("gx", "gy"), P("gx", "gy"), P("gx", "gy"), P(None, "gx", "gy"), P("gx", "gy")),
        out_specs=P("gx", "gy"),
        check_vma=False,
    )
```

time: 336 us -> 64.7 us (0.19)
  local copies, waits for them, and re-layouts: 92 us -> 4.44 us
  starting transfers between devices: 79 us -> 9.05 us
  other arithmetic: 46.9 us -> 0 us
  loops' own time: 44.3 us -> 0 us
  waiting for transfers between devices: 30.3 us -> 6.04 us
  Pallas kernels: 0 us -> 13.9 us
  blocking collectives: 41.1 us -> 30.8 us
    dynamic_update_slice x1680 -> x0, local copies, waits for them, and re-layouts: 59.2 us -> none  [the longest x1536 57.8 us: factor(): lax.scan(advance, jnp.zeros_like(main_diag[0]), (sub_diag, main_diag, sup...]
    all_to_all x6 -> x0, starting transfers between devices: 47.4 us -> none  [the longest x2 16.1 us: local(): lax.all_to_all(source.T, 'gy', split_axis=1, concat_axis=1, tiled=True)]
    another operation x22 -> x0, loops' own time: 44.3 us -> none  [the longest x6 16.7 us: substitute(): lax.scan(backward, jnp.zeros_like(source[0]), (ratios, partial_sol), reve...]
    all_to_all x6 -> x0, waiting for transfers between devices: 28.3 us -> none  [the longest x2 14 us: local(): lax.all_to_all(source.T, 'gy', split_axis=1, concat_axis=1, tiled=True)]
    ppermute x12 -> x8, starting transfers between devices: 31.6 us -> 9.05 us  [the longest x6 5.7 us: share_x(): lax.ppermute(sent, 'gx', [(i, (i + by) % COUNT_X) for i in range(COUNT_X)])]
    all_gather x2 -> x0, blocking collectives: 19.3 us -> none  [local(): gathered = lax.all_gather(solve_own_rel[None], 'gx', axis=0, tiled=True)]
    mul x919 -> x0, other arithmetic: 17.2 us -> none  [the longest x512 10.2 us: forward(): new_value = (source_row - sub_row * prev_value) * pivot_row]
    another operation x316 -> x0, local copies, waits for them, and re-layouts: 17 us -> none
where the time goes in v1:
time: 64.7 us; the launch traced here: 64.2 us
  blocking collectives  30.8 us (48%)
  Pallas kernels  13.9 us (21%)
  starting transfers between devices  9.05 us (14%)
  waiting for transfers between devices  6.04 us (9%)
  local copies, waits for them, and re-layouts  4.44 us (7%)
    all_to_all x2, blocking collectives, share_y(): lax.all_to_all(copies, 'gy', split_axis=0, concat_axis=0, tiled=True)  30.8 us
    pallas_call x7, Pallas kernels, call(): pl.pallas_call(body, out_shape=[jax.ShapeDtypeStruct((rows, LANES), jnp.f...  13.9 us
    ppermute x6, waiting for transfers between devices, share_x(): lax.ppermute(sent, 'gx', [(i, (i + by) % COUNT_X) for i in range(COUNT_X)])  6.03 us
    ppermute x6, starting transfers between devices, share_x(): lax.ppermute(sent, 'gx', [(i, (i + by) % COUNT_X) for i in range(COUNT_X)])  5.7 us
    unnamed x24, local copies, waits for them, and re-layouts  3.74 us
    ppermute x1, starting transfers between devices, local(): outside = lax.ppermute(outside, 'gy', pairs)  1.92 us
    ppermute x1, starting transfers between devices, local(): inside = lax.ppermute(inside, 'gy', [(i, i ^ 1) for i in range(COUNT_Y)])  1.42 us
  transfers between devices with their start and end apart: 8, of which 5 were waited for; matrix products, arithmetic and copies ran while one was open for 0% of the time, Pallas kernels for 3%

profile of v1, /device:TPU:1, one launch (start us, length us, event | category | flops | bytes accessed | tf_op | source)
XLA Modules:
  0.0 64.2 jit_solution(10444310940328881703)
XLA Ops:
  0.0 1.6 %prepare.1 = (f32[128,128]{1,0:T(8,128)}, f32[128,128]{1,0:T(8,128)}, f32[2,128]{1,0:T(2,128)}, f32[2,128]{1,0:T(2,128)}) custom-call(f32[128,128]{1,0:T(8,128)} %v.1, f32[128,128]{1,0:T(8,128)} %warm.3), custom_call_target="tpu_custom_call" | custom-call | tf_op jit(solution)/shard_map/prepare/pallas_call | solution.py:466
  1.6 0.7 %copy-done.11 = f32[2,128]{1,0:T(2,128)S(1)} copy-done((f32[2,128]{1,0:T(2,128)S(1)}, f32[2,128]{1,0:T(2,128)}, u32[]{:S(2)}) %copy-start.11) | copy-done | bytes 1048
  2.3 1.4 %collective-permute-start = (f32[2,128]{1,0:T(2,128)S(1)}, f32[2,128]{1,0:T(2,128)S(1)}, u32[]{:S(2)}, u32[]{:S(2)}) collective-permute-start(f32[2,128]{1,0:T(2,128)S(1)} %copy-done.11), channel_id=1, source_target_pairs={{0,1},{1,0},{2,3},{3,2},{4,5},{5,4},{6,7},{7,6},{8,9},{9,8},{10,11... | collective-permute-start | bytes 3080 | tf_op jit(solution)/shard_map/ppermute | solution.py:494
  3.7 1.9 %collective-permute-start.1 = (f32[2,128]{1,0:T(2,128)S(1)}, f32[2,128]{1,0:T(2,128)S(1)}, u32[]{:S(2)}, u32[]{:S(2)}) collective-permute-start(f32[2,128]{1,0:T(2,128)S(1)} %copy-done.10), channel_id=1, source_target_pairs={{0,31},{1,2},{2,1},{3,4},{4,3},{5,6},{6,5},{7,8},{8,7},{9,10},{10,... | collective-permute-start | bytes 3080 | tf_op jit(solution)/shard_map/ppermute | solution.py:496
  5.7 1.9 %coefficients.1 = (f32[432,128]{1,0:T(8,128)}, f32[432,128]{1,0:T(8,128)}, f32[128,128]{1,0:T(8,128)}, f32[8,128]{1,0:T(8,128)}, f32[8,128]{1,0:T(8,128)}, /*index=5*/f32[128,128]{1,0:T(8,128)}, f32[8,128]{1,0:T(8,128)}) custom-call(f32[128,128]{1,0:T(8,128)} %cap.5, f32[128,128]{1,0:T(8,128)} %warm.3, f32[128,128]{1,0:T(8,128)} %get-tuple-element.31.warm_t, ...), custom_call_target="tpu_custom_call" | custom-call | tf_op jit(solution)/shard_map/coefficients/pallas_call | solution.py:466
  7.6 0.0 collective-permute-done.inside
  7.6 0.5 copy-done.4
  8.2 0.0 copy-done.6
  8.2 2.0 %begin.1 = (f32[128,128]{1,0:T(8,128)}, f32[128,128]{1,0:T(8,128)}, f32[8,128]{1,0:T(8,128)}, f32[8,128]{1,0:T(8,128)}) custom-call(f32[128,128]{1,0:T(8,128)} %get-tuple-element.30.v_t, f32[128,128]{1,0:T(8,128)} %get-tuple-element.31.warm_t, f32[128,128]{1,0:T(8,128)} %get-tuple-element.32.cap_t, f32[2,128,128]{2,1,0:T(8,128)} %load.7, ...), custom_call_target="tpu_custom_call" | custom-call | tf_op jit(solution)/shard_map/begin/pallas_call | solution.py:466
  10.2 2.5 %collective-permute-start.4 = (f32[8,128]{1,0:T(8,128)}, f32[8,128]{1,0:T(8,128)S(1)}, u32[]{:S(2)}, u32[]{:S(2)}) collective-permute-start(f32[8,128]{1,0:T(8,128)} %get-tuple-element.40.own), channel_id=1, source_target_pairs={{0,96},{32,0},{64,32},{96,64},{1,97},{33,1},{65,33},{97,65},{2,98}... | collective-permute-start | bytes 12296 | tf_op jit(solution)/shard_map/ppermute | solution.py:478
  12.6 0.5 collective-permute-start.3
  13.2 0.6 collective-permute-start.2
  13.8 3.0 %collective-permute-done.3.two = f32[8,128]{1,0:T(8,128)S(1)} collective-permute-done((f32[8,128]{1,0:T(8,128)}, f32[8,128]{1,0:T(8,128)S(1)}, u32[]{:S(2)}, u32[]{:S(2)}) %collective-permute-start.3) | collective-permute-done | bytes 4128 | tf_op jit(solution)/shard_map/ppermute | solution.py:478
  16.8 0.2 collective-permute-done.2.one
  17.0 0.4 copy-done.1
  17.4 0.2 copy-done.2
  17.6 2.1 %first_x.1 = (f32[192,128]{1,0:T(8,128)}, f32[128,128]{1,0:T(8,128)}, f32[128,128]{1,0:T(8,128)}, f32[8,128]{1,0:T(8,128)}) custom-call(f32[8,128]{1,0:T(8,128)} %get-tuple-element.40.own, f32[8,128]{1,0:T(8,128)} %copy-done.2, f32[8,128]{1,0:T(8,128)} %copy-done.1, f32[8,128]{1,0:T(8,128)} %copy-done, f32[128,128]{1,0:T(8,128)} %cap.5, ...), custom_call_target="tpu_custom_call" | custom-call | tf_op jit(solution)/shard_map/first_x/pallas_call | solution.py:466
  19.7 0.7 %broadcast_in_dim.4 = f32[32,8,128]{2,1,0:T(8,128)S(1)} broadcast(f32[8,128]{1,0:T(8,128)} %get-tuple-element.45), dimensions={1,2} | broadcast | bytes 135168 | tf_op jit(solution)/shard_map/broadcast_in_dim | solution.py:485
  20.4 18.1 %all_to_all.10 = f32[32,8,128]{2,1,0:T(8,128)} all-to-all(f32[32,8,128]{2,1,0:T(8,128)S(1)} %broadcast_in_dim.4), channel_id=1, replica_groups=mesh['gx'=4,'gy'=32] {'gy'}, dimensions={0} | all-to-all | bytes 262144 | tf_op jit(solution)/shard_map/all_to_all | solution.py:486
  38.5 2.2 %first_y.1 = (f32[248,128]{1,0:T(8,128)}, f32[128,128]{1,0:T(8,128)}, f32[128,128]{1,0:T(8,128)}, f32[2,128]{1,0:T(2,128)}) custom-call(f32[256,128]{1,0:T(8,128)} %bitcast.2, f32[128,128]{1,0:T(8,128)} %get-tuple-element.32.cap_t, f32[2,128,128]{2,1,0:T(8,128)} %load.7, f32[128,128]{1,0:T(8,128)} %get-tuple-element.46.s_in, ...), custom_call_target="tpu_custom_call" | custom-call | tf_op jit(solution)/shard_map/first_y/pallas_call | solution.py:466
  40.7 0.7 %copy-done.3 = f32[2,128]{1,0:T(2,128)S(1)} copy-done((f32[2,128]{1,0:T(2,128)S(1)}, f32[2,128]{1,0:T(2,128)}, u32[]{:S(2)}) %copy-start.3) | copy-done | bytes 1048
  41.4 0.3 collective-permute-start.7
  41.7 0.9 %collective-permute-start.6 = (f32[2,128]{1,0:T(2,128)S(1)}, f32[2,128]{1,0:T(2,128)S(1)}, u32[]{:S(2)}, u32[]{:S(2)}) collective-permute-start(f32[2,128]{1,0:T(2,128)S(1)} %copy-done.3), channel_id=1, source_target_pairs={{0,64},{32,96},{64,0},{96,32},{1,65},{33,97},{65,1},{97,33},{2,66}... | collective-permute-start | bytes 3080 | tf_op jit(solution)/shard_map/ppermute | solution.py:478
  42.6 0.9 %collective-permute-start.5 = (f32[2,128]{1,0:T(2,128)S(1)}, f32[2,128]{1,0:T(2,128)S(1)}, u32[]{:S(2)}, u32[]{:S(2)}) collective-permute-start(f32[2,128]{1,0:T(2,128)S(1)} %copy-done.3), channel_id=1, source_target_pairs={{0,32},{32,64},{64,96},{96,0},{1,33},{33,65},{65,97},{97,1},{2,34}... | collective-permute-start | bytes 3080 | tf_op jit(solution)/shard_map/ppermute | solution.py:478
  43.5 0.3 collective-permute-done.7.three
  43.8 1.8 %collective-permute-done.6.two = f32[2,128]{1,0:T(2,128)S(1)} collective-permute-done((f32[2,128]{1,0:T(2,128)S(1)}, f32[2,128]{1,0:T(2,128)S(1)}, u32[]{:S(2)}, u32[]{:S(2)}) %collective-permute-start.6) | collective-permute-done | bytes 1056 | tf_op jit(solution)/shard_map/ppermute | solution.py:478
  45.7 0.6 collective-permute-done.5.one
  46.3 0.6 copy-done.8
  46.8 2.1 %second_x.1 = (f32[128,128]{1,0:T(8,128)}, f32[2,128]{1,0:T(2,128)}) custom-call(f32[2,128]{1,0:T(2,128)} %get-tuple-element.48.own, f32[2,128]{1,0:T(2,128)} %copy-done.8, f32[2,128]{1,0:T(2,128)} %copy-done.7, f32[2,128]{1,0:T(2,128)} %copy-done.5, f32[128,128]{1,0:T(8,128)} %cap.5, f32[2,128,128]{2,1,0:T(8,128)} %load.7, ...), custom_call_target="tpu_custom_call" | custom-call | tf_op jit(solution)/shard_map/second_x/pallas_call | solution.py:466
  48.9 0.7 %copy-done.9 = f32[2,128]{1,0:T(2,128)S(1)} copy-done((f32[2,128]{1,0:T(2,128)S(1)}, f32[2,128]{1,0:T(2,128)}, u32[]{:S(2)}) %copy-start.9) | copy-done | bytes 1048
  49.6 12.7 %all_to_all.11 = f32[32,2,128]{2,1,0:T(2,128)} all-to-all(f32[32,2,128]{2,1,0:T(2,128)S(1)} %broadcast_in_dim.5), channel_id=1, replica_groups=mesh['gx'=4,'gy'=32] {'gy'}, dimensions={0} | all-to-all | bytes 65536 | tf_op jit(solution)/shard_map/all_to_all | solution.py:486
  62.3 1.9 %second_y.1 = f32[128,128]{1,0:T(8,128)} custom-call(f32[64,128]{1,0:T(8,128)} %bitcast.3, f32[128,128]{1,0:T(8,128)} %get-tuple-element.53.f_in, f32[432,128]{1,0:T(8,128)} %get-tuple-element.43.y_ref, f32[248,128]{1,0:T(8,128)} %get-tuple-element.54.y_join), custom_call_target="tpu_custom_call" | custom-call | tf_op jit(solution)/shard_map/second_y/pallas_call | solution.py:466
  (19 shorter events, 0.0 us)
Async XLA Ops:
  1.6 0.7 %copy-start.11 = (f32[2,128]{1,0:T(2,128)S(1)}, f32[2,128]{1,0:T(2,128)}, u32[]{:S(2)}) copy-start(f32[2,128]{1,0:T(2,128)} %get-tuple-element.33) | copy-start | bytes 3076
  2.3 1.4 %copy-start.10 = (f32[2,128]{1,0:T(2,128)S(1)}, f32[2,128]{1,0:T(2,128)}, u32[]{:S(2)}) copy-start(f32[2,128]{1,0:T(2,128)} %get-tuple-element.34) | copy-start | bytes 3076
  2.3 5.3 %collective-permute-start = (f32[2,128]{1,0:T(2,128)S(1)}, f32[2,128]{1,0:T(2,128)S(1)}, u32[]{:S(2)}, u32[]{:S(2)}) collective-permute-start(f32[2,128]{1,0:T(2,128)S(1)} %copy-done.11), channel_id=1, source_target_pairs={{0,1},{1,0},{2,3},{3,2},{4,5},{5,4},{6,7},{7,6},{8,9},{9,8},{10,11... | collective-permute-start | bytes 3080 | tf_op jit(solution)/shard_map/ppermute | solution.py:494
  3.7 3.9 %collective-permute-start.1 = (f32[2,128]{1,0:T(2,128)S(1)}, f32[2,128]{1,0:T(2,128)S(1)}, u32[]{:S(2)}, u32[]{:S(2)}) collective-permute-start(f32[2,128]{1,0:T(2,128)S(1)} %copy-done.10), channel_id=1, source_target_pairs={{0,31},{1,2},{2,1},{3,4},{4,3},{5,6},{6,5},{7,8},{8,7},{9,10},{10,... | collective-permute-start | bytes 3080 | tf_op jit(solution)/shard_map/ppermute | solution.py:496
  7.6 0.6 copy-start.4
  7.6 0.6 copy-start.6
  10.2 3.6 %collective-permute-start.4 = (f32[8,128]{1,0:T(8,128)}, f32[8,128]{1,0:T(8,128)S(1)}, u32[]{:S(2)}, u32[]{:S(2)}) collective-permute-start(f32[8,128]{1,0:T(8,128)} %get-tuple-element.40.own), channel_id=1, source_target_pairs={{0,96},{32,0},{64,32},{96,64},{1,97},{33,1},{65,33},{97,65},{2,98}... | collective-permute-start | bytes 12296 | tf_op jit(solution)/shard_map/ppermute | solution.py:478
  12.6 4.2 %collective-permute-start.3 = (f32[8,128]{1,0:T(8,128)}, f32[8,128]{1,0:T(8,128)S(1)}, u32[]{:S(2)}, u32[]{:S(2)}) collective-permute-start(f32[8,128]{1,0:T(8,128)} %get-tuple-element.40.own), channel_id=1, source_target_pairs={{0,64},{32,96},{64,0},{96,32},{1,65},{33,97},{65,1},{97,33},{2,66}... | collective-permute-start | bytes 12296 | tf_op jit(solution)/shard_map/ppermute | solution.py:478
  13.2 3.9 %collective-permute-start.2 = (f32[8,128]{1,0:T(8,128)}, f32[8,128]{1,0:T(8,128)S(1)}, u32[]{:S(2)}, u32[]{:S(2)}) collective-permute-start(f32[8,128]{1,0:T(8,128)} %get-tuple-element.40.own), channel_id=1, source_target_pairs={{0,32},{32,64},{64,96},{96,0},{1,33},{33,65},{65,97},{97,1},{2,34}... | collective-permute-start | bytes 12296 | tf_op jit(solution)/shard_map/ppermute | solution.py:478
  13.8 3.3 %copy-start = (f32[8,128]{1,0:T(8,128)}, f32[8,128]{1,0:T(8,128)S(1)}, u32[]{:S(2)}) copy-start(f32[8,128]{1,0:T(8,128)S(1)} %collective-permute-done.4.three) | copy-start | bytes 12292
  16.8 0.6 copy-start.1
  17.0 0.6 copy-start.2
  40.7 0.7 %copy-start.3 = (f32[2,128]{1,0:T(2,128)S(1)}, f32[2,128]{1,0:T(2,128)}, u32[]{:S(2)}) copy-start(f32[2,128]{1,0:T(2,128)} %get-tuple-element.48.own) | copy-start | bytes 3076
  41.4 2.4 %collective-permute-start.7 = (f32[2,128]{1,0:T(2,128)S(1)}, f32[2,128]{1,0:T(2,128)S(1)}, u32[]{:S(2)}, u32[]{:S(2)}) collective-permute-start(f32[2,128]{1,0:T(2,128)S(1)} %copy-done.3), channel_id=1, source_target_pairs={{0,96},{32,0},{64,32},{96,64},{1,97},{33,1},{65,33},{97,65},{2,98}... | collective-permute-start | bytes 3080 | tf_op jit(solution)/shard_map/ppermute | solution.py:478
  41.7 3.9 %collective-permute-start.6 = (f32[2,128]{1,0:T(2,128)S(1)}, f32[2,128]{1,0:T(2,128)S(1)}, u32[]{:S(2)}, u32[]{:S(2)}) collective-permute-start(f32[2,128]{1,0:T(2,128)S(1)} %copy-done.3), channel_id=1, source_target_pairs={{0,64},{32,96},{64,0},{96,32},{1,65},{33,97},{65,1},{97,33},{2,66}... | collective-permute-start | bytes 3080 | tf_op jit(solution)/shard_map/ppermute | solution.py:478
  42.6 3.6 %collective-permute-start.5 = (f32[2,128]{1,0:T(2,128)S(1)}, f32[2,128]{1,0:T(2,128)S(1)}, u32[]{:S(2)}, u32[]{:S(2)}) collective-permute-start(f32[2,128]{1,0:T(2,128)S(1)} %copy-done.3), channel_id=1, source_target_pairs={{0,32},{32,64},{64,96},{96,0},{1,33},{33,65},{65,97},{97,1},{2,34}... | collective-permute-start | bytes 3080 | tf_op jit(solution)/shard_map/ppermute | solution.py:478
  43.8 2.5 %copy-start.5 = (f32[2,128]{1,0:T(2,128)}, f32[2,128]{1,0:T(2,128)S(1)}, u32[]{:S(2)}) copy-start(f32[2,128]{1,0:T(2,128)S(1)} %collective-permute-done.7.three) | copy-start | bytes 3076
  45.7 0.6 copy-start.7
  46.3 0.6 copy-start.8
  48.9 0.7 %copy-start.9 = (f32[2,128]{1,0:T(2,128)S(1)}, f32[2,128]{1,0:T(2,128)}, u32[]{:S(2)}) copy-start(f32[2,128]{1,0:T(2,128)} %get-tuple-element.52) | copy-start | bytes 3076

commit v2 on v1

--- a/solution.py
+++ b/solution.py
@@ -458,14 +458,19 @@
     out[...] = flat[...].T
 
 
-def call(body, shapes, args, scratch=(), scalars=()):
+def call(body, shapes, args, scratch=(), scalars=(), near=True):
+    args = [
+        x if n in scalars else pltpu.with_memory_space_constraint(x, pltpu.VMEM)
+        for n, x in enumerate(args)
+    ]
+    made = pltpu.VMEM if near else jax.ShapeDtypeStruct
     specs = [
         pl.BlockSpec(memory_space=pltpu.SMEM if n in scalars else pltpu.VMEM)
         for n in range(len(args))
     ]
     return pl.pallas_call(
         body,
-        out_shape=[jax.ShapeDtypeStruct((rows, LANES), jnp.float32) for rows in shapes],
+        out_shape=[made((rows, LANES), jnp.float32) for rows in shapes],
         in_specs=specs,
         out_specs=[pl.BlockSpec(memory_space=pltpu.VMEM)] * len(shapes),
         scratch_shapes=[pltpu.VMEM((rows, LANES), jnp.float32) for rows in scratch],
@@ -531,6 +536,7 @@
         (ROWS,),
         (share_y(sent), f, y_ref, y_join),
         scratch=(2 * Y_DEPTH * SUB, ROWS),
+        near=False,
     )
     return drop
 

time: 64.7 us -> 51.6 us (0.80)
  Pallas kernels: 13.9 us -> 2.87 us
  local copies, waits for them, and re-layouts: 4.44 us -> 1.75 us
  waiting for transfers between devices: 6.04 us -> 6.93 us
    pallas_call x7, Pallas kernels: 13.9 us -> 2.87 us  [call(): pl.pallas_call(body, out_shape=[made((rows, LANES), jnp.float32) for rows...]
    unnamed x24 -> x8, local copies, waits for them, and re-layouts: 3.74 us -> 1.72 us
    ppermute x1, waiting for transfers between devices: 0.01 us -> 0.71 us  [local(): outside = lax.ppermute(outside, 'gy', pairs)]
    broadcast_in_dim x2, local copies, waits for them, and re-layouts: 0.7 us -> 0.03 us  [share_y(): copies = jnp.broadcast_to(sent[None], (COUNT_Y, rows, LANES))]
  transfers between devices with their start and end apart: 8 -> 8, of which waited for: 5 -> 6; matrix products, arithmetic and copies ran while one was open for 0% -> 0% of each run, Pallas kernels for 3% -> 2%
where the time goes in v2:
time: 51.6 us; the launch traced here: 51.3 us
  blocking collectives  30.9 us (60%)
  starting transfers between devices  8.78 us (17%)
  waiting for transfers between devices  6.93 us (13%)
  Pallas kernels  2.87 us (6%)
  local copies, waits for them, and re-layouts  1.75 us (3%)
    all_to_all x2, blocking collectives, share_y(): lax.all_to_all(copies, 'gy', split_axis=0, concat_axis=0, tiled=True)  30.9 us
    ppermute x6, waiting for transfers between devices, share_x(): lax.ppermute(sent, 'gx', [(i, (i + by) % COUNT_X) for i in range(COUNT_X)])  6.22 us
    ppermute x6, starting transfers between devices, share_x(): lax.ppermute(sent, 'gx', [(i, (i + by) % COUNT_X) for i in range(COUNT_X)])  5.92 us
    pallas_call x7, Pallas kernels, call(): pl.pallas_call(body, out_shape=[made((rows, LANES), jnp.float32) for rows...  2.87 us
    unnamed x8, local copies, waits for them, and re-layouts  1.72 us
    ppermute x1, starting transfers between devices, local(): inside = lax.ppermute(inside, 'gy', [(i, i ^ 1) for i in range(COUNT_Y)])  1.5 us
    ppermute x1, starting transfers between devices, local(): outside = lax.ppermute(outside, 'gy', pairs)  1.36 us
  transfers between devices with their start and end apart: 8, of which 6 were waited for; matrix products, arithmetic and copies ran while one was open for 0% of the time, Pallas kernels for 2%

profile of v2, /device:TPU:1, one launch (start us, length us, event | category | flops | bytes accessed | tf_op | source)
XLA Modules:
  0.0 51.3 jit_solution(15250977237952806019)
XLA Ops:
  0.0 0.0 copy-start.1
  0.0 0.0 copy-start.2
  0.0 0.9 %copy-done.2 = f32[128,128]{1,0:T(8,128)S(1)} copy-done((f32[128,128]{1,0:T(8,128)S(1)}, f32[128,128]{1,0:T(8,128)}, u32[]{:S(2)}) %copy-start.2) | copy-done | bytes 65560
  0.9 0.8 %copy-done.3 = f32[128,128]{1,0:T(8,128)S(1)} copy-done((f32[128,128]{1,0:T(8,128)S(1)}, f32[128,128]{1,0:T(8,128)}, u32[]{:S(2)}) %copy-start.3) | copy-done | bytes 65560
  1.7 0.1 prepare.1
  1.8 0.0 copy-start
  1.8 1.5 %collective-permute-start = (f32[2,128]{1,0:T(2,128)S(1)}, f32[2,128]{1,0:T(2,128)S(1)}, u32[]{:S(2)}, u32[]{:S(2)}) collective-permute-start(f32[2,128]{1,0:T(2,128)S(1)} %get-tuple-element.33), channel_id=1, source_target_pairs={{0,1},{1,0},{2,3},{3,2},{4,5},{5,4},{6,7},{7,6},{8,9},{9,8},{10,11... | collective-permute-start | bytes 3080 | tf_op jit(solution)/shard_map/ppermute | solution.py:499
  3.3 1.4 %collective-permute-start.1 = (f32[2,128]{1,0:T(2,128)S(1)}, f32[2,128]{1,0:T(2,128)S(1)}, u32[]{:S(2)}, u32[]{:S(2)}) collective-permute-start(f32[2,128]{1,0:T(2,128)S(1)} %get-tuple-element.34), channel_id=1, source_target_pairs={{0,31},{1,2},{2,1},{3,4},{4,3},{5,6},{6,5},{7,8},{8,7},{9,10},{10,... | collective-permute-start | bytes 3080 | tf_op jit(solution)/shard_map/ppermute | solution.py:501
  4.7 0.0 copy-done.1
  4.7 0.9 %coefficients.1 = (f32[432,128]{1,0:T(8,128)S(1)}, f32[432,128]{1,0:T(8,128)S(1)}, f32[128,128]{1,0:T(8,128)S(1)}, f32[8,128]{1,0:T(8,128)S(1)}, f32[8,128]{1,0:...) custom-call(f32[128,128]{1,0:T(8,128)S(1)} %copy-done.1, f32[128,128]{1,0:T(8,128)S(1)} %copy-done.2, ...), custom_call_target="tpu_custom_call" | custom-call | tf_op jit(solution)/shard_map/coefficients/pallas_call | solution.py:471
  5.6 0.0 collective-permute-done.inside
  5.6 0.7 %collective-permute-done.1.outside = f32[2,128]{1,0:T(2,128)S(1)} collective-permute-done((f32[2,128]{1,0:T(2,128)S(1)}, f32[2,128]{1,0:T(2,128)S(1)}, u32[]{:S(2)}, u32[]{:S(2)}) %collective-permute-start.1) | collective-permute-done | bytes 1056 | tf_op jit(solution)/shard_map/ppermute | solution.py:501
  6.3 0.0 copy-done
  6.3 0.2 begin.1
  6.5 2.6 %collective-permute-start.4 = (f32[8,128]{1,0:T(8,128)S(1)}, f32[8,128]{1,0:T(8,128)S(1)}, u32[]{:S(2)}, u32[]{:S(2)}) collective-permute-start(f32[8,128]{1,0:T(8,128)S(1)} %get-tuple-element.40.own), channel_id=1, source_target_pairs={{0,96},{32,0},{64,32},{96,64},{1,97},{33,1},{65,33},{97,65},{2,98}... | collective-permute-start | bytes 12296 | tf_op jit(solution)/shard_map/ppermute | solution.py:483
  9.2 0.5 %collective-permute-start.3 = (f32[8,128]{1,0:T(8,128)S(1)}, f32[8,128]{1,0:T(8,128)S(1)}, u32[]{:S(2)}, u32[]{:S(2)}) collective-permute-start(f32[8,128]{1,0:T(8,128)S(1)} %get-tuple-element.40.own), channel_id=1, source_target_pairs={{0,64},{32,96},{64,0},{96,32},{1,65},{33,97},{65,1},{97,33},{2,66}... | collective-permute-start | bytes 12296 | tf_op jit(solution)/shard_map/ppermute | solution.py:483
  9.7 0.6 %collective-permute-start.2 = (f32[8,128]{1,0:T(8,128)S(1)}, f32[8,128]{1,0:T(8,128)S(1)}, u32[]{:S(2)}, u32[]{:S(2)}) collective-permute-start(f32[8,128]{1,0:T(8,128)S(1)} %get-tuple-element.40.own), channel_id=1, source_target_pairs={{0,32},{32,64},{64,96},{96,0},{1,33},{33,65},{65,97},{97,1},{2,34}... | collective-permute-start | bytes 12296 | tf_op jit(solution)/shard_map/ppermute | solution.py:483
  10.3 0.0 collective-permute-done.4.three
  10.3 2.8 %collective-permute-done.3.two = f32[8,128]{1,0:T(8,128)S(1)} collective-permute-done((f32[8,128]{1,0:T(8,128)S(1)}, f32[8,128]{1,0:T(8,128)S(1)}, u32[]{:S(2)}, u32[]{:S(2)}) %collective-permute-start.3) | collective-permute-done | bytes 4128 | tf_op jit(solution)/shard_map/ppermute | solution.py:483
  13.1 0.2 collective-permute-done.2.one
  13.4 0.3 first_x.1
  13.6 18.8 %all_to_all.10 = f32[32,8,128]{2,1,0:T(8,128)S(1)} all-to-all(f32[32,8,128]{2,1,0:T(8,128)S(1)} %broadcast_in_dim.4), channel_id=1, replica_groups=mesh['gx'=4,'gy'=32] {'gy'}, dimensions={0} | all-to-all | bytes 262144 | tf_op jit(solution)/shard_map/all_to_all | solution.py:491
  32.4 0.3 first_y.1
  32.7 0.4 collective-permute-start.7
  33.1 1.0 %collective-permute-start.6 = (f32[2,128]{1,0:T(2,128)S(1)}, f32[2,128]{1,0:T(2,128)S(1)}, u32[]{:S(2)}, u32[]{:S(2)}) collective-permute-start(f32[2,128]{1,0:T(2,128)S(1)} %get-tuple-element.48.own), channel_id=1, source_target_pairs={{0,64},{32,96},{64,0},{96,32},{1,65},{33,97},{65,1},{97,33},{2,66}... | collective-permute-start | bytes 3080 | tf_op jit(solution)/shard_map/ppermute | solution.py:483
  34.1 0.8 %collective-permute-start.5 = (f32[2,128]{1,0:T(2,128)S(1)}, f32[2,128]{1,0:T(2,128)S(1)}, u32[]{:S(2)}, u32[]{:S(2)}) collective-permute-start(f32[2,128]{1,0:T(2,128)S(1)} %get-tuple-element.48.own), channel_id=1, source_target_pairs={{0,32},{32,64},{64,96},{96,0},{1,33},{33,65},{65,97},{97,1},{2,34}... | collective-permute-start | bytes 3080 | tf_op jit(solution)/shard_map/ppermute | solution.py:483
  34.9 0.3 collective-permute-done.7.three
  35.2 1.8 %collective-permute-done.6.two = f32[2,128]{1,0:T(2,128)S(1)} collective-permute-done((f32[2,128]{1,0:T(2,128)S(1)}, f32[2,128]{1,0:T(2,128)S(1)}, u32[]{:S(2)}, u32[]{:S(2)}) %collective-permute-start.6) | collective-permute-done | bytes 1056 | tf_op jit(solution)/shard_map/ppermute | solution.py:483
  37.1 1.0 %collective-permute-done.5.one = f32[2,128]{1,0:T(2,128)S(1)} collective-permute-done((f32[2,128]{1,0:T(2,128)S(1)}, f32[2,128]{1,0:T(2,128)S(1)}, u32[]{:S(2)}, u32[]{:S(2)}) %collective-permute-start.5) | collective-permute-done | bytes 1056 | tf_op jit(solution)/shard_map/ppermute | solution.py:483
  38.1 0.2 second_x.1
  38.3 12.2 %all_to_all.11 = f32[32,2,128]{2,1,0:T(2,128)S(1)} all-to-all(f32[32,2,128]{2,1,0:T(2,128)S(1)} %broadcast_in_dim.5), channel_id=1, replica_groups=mesh['gx'=4,'gy'=32] {'gy'}, dimensions={0} | all-to-all | bytes 65536 | tf_op jit(solution)/shard_map/all_to_all | solution.py:491
  50.5 0.8 %second_y.1 = f32[128,128]{1,0:T(8,128)} custom-call(f32[64,128]{1,0:T(8,128)S(1)} %bitcast.3, f32[128,128]{1,0:T(8,128)S(1)} %get-tuple-element.53.f_in, f32[432,128]{1,0:T(8,128)S(1)} %get-tuple-element.43.y_ref, f32[248,128]{1,0:T(8,128)S(1)} %get-tuple-element.54.y_join), custom_call_target="tpu_custom_call" | custom-call | tf_op jit(solution)/shard_map/second_y/pallas_call | solution.py:471
  (3 shorter events, 0.0 us)
Async XLA Ops:
  0.0 4.7 %copy-start.1 = (f32[128,128]{1,0:T(8,128)S(1)}, f32[128,128]{1,0:T(8,128)}, u32[]{:S(2)}) copy-start(f32[128,128]{1,0:T(8,128)} %cap.5) | copy-start | bytes 196612
  0.0 0.9 %copy-start.2 = (f32[128,128]{1,0:T(8,128)S(1)}, f32[128,128]{1,0:T(8,128)}, u32[]{:S(2)}) copy-start(f32[128,128]{1,0:T(8,128)} %warm.3) | copy-start | bytes 196612
  0.9 0.8 %copy-start.3 = (f32[128,128]{1,0:T(8,128)S(1)}, f32[128,128]{1,0:T(8,128)}, u32[]{:S(2)}) copy-start(f32[128,128]{1,0:T(8,128)} %v.1) | copy-start | bytes 196612
  1.8 4.5 %copy-start = (f32[2,128,128]{2,1,0:T(8,128)S(1)}, f32[2,128,128]{2,1,0:T(8,128)}, u32[]{:S(2)}) copy-start(f32[2,128,128]{2,1,0:T(8,128)} %load.7) | copy-start | bytes 393220
  1.8 3.8 %collective-permute-start = (f32[2,128]{1,0:T(2,128)S(1)}, f32[2,128]{1,0:T(2,128)S(1)}, u32[]{:S(2)}, u32[]{:S(2)}) collective-permute-start(f32[2,128]{1,0:T(2,128)S(1)} %get-tuple-element.33), channel_id=1, source_target_pairs={{0,1},{1,0},{2,3},{3,2},{4,5},{5,4},{6,7},{7,6},{8,9},{9,8},{10,11... | collective-permute-start | bytes 3080 | tf_op jit(solution)/shard_map/ppermute | solution.py:499
  3.3 3.0 %collective-permute-start.1 = (f32[2,128]{1,0:T(2,128)S(1)}, f32[2,128]{1,0:T(2,128)S(1)}, u32[]{:S(2)}, u32[]{:S(2)}) collective-permute-start(f32[2,128]{1,0:T(2,128)S(1)} %get-tuple-element.34), channel_id=1, source_target_pairs={{0,31},{1,2},{2,1},{3,4},{4,3},{5,6},{6,5},{7,8},{8,7},{9,10},{10,... | collective-permute-start | bytes 3080 | tf_op jit(solution)/shard_map/ppermute | solution.py:501
  6.5 3.8 %collective-permute-start.4 = (f32[8,128]{1,0:T(8,128)S(1)}, f32[8,128]{1,0:T(8,128)S(1)}, u32[]{:S(2)}, u32[]{:S(2)}) collective-permute-start(f32[8,128]{1,0:T(8,128)S(1)} %get-tuple-element.40.own), channel_id=1, source_target_pairs={{0,96},{32,0},{64,32},{96,64},{1,97},{33,1},{65,33},{97,65},{2,98}... | collective-permute-start | bytes 12296 | tf_op jit(solution)/shard_map/ppermute | solution.py:483
  9.2 4.0 %collective-permute-start.3 = (f32[8,128]{1,0:T(8,128)S(1)}, f32[8,128]{1,0:T(8,128)S(1)}, u32[]{:S(2)}, u32[]{:S(2)}) collective-permute-start(f32[8,128]{1,0:T(8,128)S(1)} %get-tuple-element.40.own), channel_id=1, source_target_pairs={{0,64},{32,96},{64,0},{96,32},{1,65},{33,97},{65,1},{97,33},{2,66}... | collective-permute-start | bytes 12296 | tf_op jit(solution)/shard_map/ppermute | solution.py:483
  9.7 3.7 %collective-permute-start.2 = (f32[8,128]{1,0:T(8,128)S(1)}, f32[8,128]{1,0:T(8,128)S(1)}, u32[]{:S(2)}, u32[]{:S(2)}) collective-permute-start(f32[8,128]{1,0:T(8,128)S(1)} %get-tuple-element.40.own), channel_id=1, source_target_pairs={{0,32},{32,64},{64,96},{96,0},{1,33},{33,65},{65,97},{97,1},{2,34}... | collective-permute-start | bytes 12296 | tf_op jit(solution)/shard_map/ppermute | solution.py:483
  32.7 2.5 %collective-permute-start.7 = (f32[2,128]{1,0:T(2,128)S(1)}, f32[2,128]{1,0:T(2,128)S(1)}, u32[]{:S(2)}, u32[]{:S(2)}) collective-permute-start(f32[2,128]{1,0:T(2,128)S(1)} %get-tuple-element.48.own), channel_id=1, source_target_pairs={{0,96},{32,0},{64,32},{96,64},{1,97},{33,1},{65,33},{97,65},{2,98}... | collective-permute-start | bytes 3080 | tf_op jit(solution)/shard_map/ppermute | solution.py:483
  33.1 3.9 %collective-permute-start.6 = (f32[2,128]{1,0:T(2,128)S(1)}, f32[2,128]{1,0:T(2,128)S(1)}, u32[]{:S(2)}, u32[]{:S(2)}) collective-permute-start(f32[2,128]{1,0:T(2,128)S(1)} %get-tuple-element.48.own), channel_id=1, source_target_pairs={{0,64},{32,96},{64,0},{96,32},{1,65},{33,97},{65,1},{97,33},{2,66}... | collective-permute-start | bytes 3080 | tf_op jit(solution)/shard_map/ppermute | solution.py:483
  34.1 3.9 %collective-permute-start.5 = (f32[2,128]{1,0:T(2,128)S(1)}, f32[2,128]{1,0:T(2,128)S(1)}, u32[]{:S(2)}, u32[]{:S(2)}) collective-permute-start(f32[2,128]{1,0:T(2,128)S(1)} %get-tuple-element.48.own), channel_id=1, source_target_pairs={{0,32},{32,64},{64,96},{96,0},{1,33},{33,65},{65,97},{97,1},{2,34}... | collective-permute-start | bytes 3080 | tf_op jit(solution)/shard_map/ppermute | solution.py:483

commit v3 on v2

--- a/solution.py
+++ b/solution.py
@@ -169,7 +169,7 @@
     count = own.shape[0]
     joined[pl.ds(pl.multiple_of(place * SUB, SUB), count), :] = own[...]
     for n, other in enumerate(others):
-        source = lax.rem(place + COUNT_X - (n + 1), COUNT_X)
+        source = jnp.bitwise_xor(place, n + 1)
         joined[pl.ds(pl.multiple_of(source * SUB, SUB), count), :] = other[...]
 
 
@@ -299,14 +299,15 @@
     return spread(found[pl.ds(at, 1), :]), spread(found[pl.ds(at + SUB, 1), :])
 
 
-def prepare(v, warm, v_t, warm_t, inside, outside):
+def put_rim(ref, v_t, warm_t, low):
+    for n, block in enumerate((v_t, warm_t)):
+        ref[n : n + 1, :] = jnp.where(low, block[0:1, :], block[ROWS - 1 : ROWS, :])
+
+
+def prepare(v, warm, v_t, warm_t, outside):
     v_t[...] = v[...].T
     warm_t[...] = warm[...].T
-    odd = lax.rem(lax.axis_index("gy"), 2) == 1
-    for n, ref in enumerate((v_t, warm_t)):
-        low, high = ref[0:1, :], ref[ROWS - 1 : ROWS, :]
-        inside[n : n + 1, :] = jnp.where(odd, low, high)
-        outside[n : n + 1, :] = jnp.where(odd, high, low)
+    put_rim(outside, v_t, warm_t, lax.rem(lax.axis_index("gy"), 2) == 0)
 
 
 def pads(flags, transposed):
@@ -315,41 +316,55 @@
     out = jnp.zeros((SUB, LANES), jnp.float32)
     for a in range(ROWS // PITCH):
         for b in range(LANES // PITCH):
-            flag = flags[b, a] if transposed else flags[a, b]
+            row, col = (b, a) if transposed else (a, b)
+            flag = spread(flags[row : row + 1, col : col + 1])
             here = (sub == a * (PITCH // DEPTH)) & (lane == b * PITCH)
             out = jnp.where(here & (flag == 1), cushion_pieces, out)
     return out
 
 
-def coefficients(cap, warm, warm_t, flags, x_ref, y_ref, cap_t, x_rows, y_rows, y_edges, y_pad):
+def put_ends(rows, own, first, end):
+    rows[...] = jnp.zeros((SUB, LANES), jnp.float32)
+    rows[2:3, :] = first
+    rows[3:4, :] = end
+    rows[4:5, :] = own
+
+
+def factor_lines_x(
+    cap, warm, v_t, warm_t, flags, x_ref, x_rows, cap_t, y_edges, y_pad, inside
+):
+    put_rim(inside, v_t, warm_t, lax.rem(lax.axis_index("gy"), 2) == 1)
     cap_t[...] = cap[...].T
-    for transposed, caps, warms, ref, rows in (
-        (False, cap, warm, x_ref, x_rows),
-        (True, cap_t, warm_t, y_ref, y_rows),
-    ):
-        admittance = yward_admittance if transposed else xward_admittance
-        temps = load_lines(warms)
-        edges = {(r, r + 1): wire(admittance, temps[r], temps[r + 1]) for r in range(DEPTH - 1)}
-        across = wire(admittance, temps[DEPTH - 1], roll(temps[0], -1))
-        pad = pads(flags, transposed)
-        if transposed:
-            store_regs(y_edges, [edges[(r, r + 1)] for r in range(DEPTH - 1)] + [across])
-            y_pad[...] = pad
-        ground = load_lines(caps)
-        ground[0] = ground[0] + pad
-        own, first, end = factor_local(ref, ground, edges, across)
-        rows[...] = jnp.zeros((SUB, LANES), jnp.float32)
-        rows[2:3, :] = first
-        rows[3:4, :] = end
-        rows[4:5, :] = own
-        if not transposed:
-            rows[5:6, :] = warms[0:1, :]
-            rows[6:7, :] = warms[ROWS - 1 : ROWS, :]
+    temps = load_lines(warm_t)
+    store_regs(
+        y_edges,
+        [wire(yward_admittance, temps[r], temps[r + 1]) for r in range(DEPTH - 1)]
+        + [wire(yward_admittance, temps[DEPTH - 1], roll(temps[0], -1))],
+    )
+    y_pad[...] = pads(flags, True)
+    temps = load_lines(warm)
+    edges = {
+        (r, r + 1): wire(xward_admittance, temps[r], temps[r + 1]) for r in range(DEPTH - 1)
+    }
+    across = wire(xward_admittance, temps[DEPTH - 1], roll(temps[0], -1))
+    ground = load_lines(cap)
+    ground[0] = ground[0] + pads(flags, False)
+    put_ends(x_rows, *factor_local(x_ref, ground, edges, across))
+    x_rows[5:6, :] = warm[0:1, :]
+    x_rows[6:7, :] = warm[ROWS - 1 : ROWS, :]
+
+
+def factor_lines_y(cap_t, y_edges, y_pad, y_ref, y_rows):
+    edges = load_regs(y_edges)
+    ground = load_lines(cap_t)
+    ground[0] = ground[0] + y_pad[...]
+    inner = {(r, r + 1): edges[r] for r in range(DEPTH - 1)}
+    put_ends(y_rows, *factor_local(y_ref, ground, inner, edges[DEPTH - 1]))
 
 
 def begin(
-    v_t, warm_t, cap_t, load, inside, outside, y_edges, y_pad, y_rows, x_ref, x_rows,
-    s_out, f_out, sent, y_rows_out, flat,
+    v_t, warm_t, cap_t, load, inside, outside, y_edges, y_pad, x_ref, x_rows,
+    s_out, f_out, sent, y_high, flat,
 ):
     sub = sublanes()
     place = lax.axis_index("gy")
@@ -362,8 +377,7 @@
     high_edge = wire(yward_admittance, warm_t[ROWS - 1 : ROWS, :], high_warm)
     low_edge = jnp.where(place > 0, low_edge, 0.0)
     high_edge = jnp.where(place < COUNT_Y - 1, high_edge, 0.0)
-    y_rows_out[...] = y_rows[...]
-    y_rows_out[5:6, :] = high_edge
+    y_high[...] = high_edge
     v = load_lines(v_t)
     cap = load_lines(cap_t)
     edges = load_regs(y_edges)
@@ -411,7 +425,7 @@
 
 
 def first_x(
-    own, one, two, three, cap, load, s_in, f_in, x_ref, y_ref, y_rows,
+    own, one, two, three, cap, load, s_in, f_in, x_ref, y_ref, y_rows, y_high,
     x_join, s_out, f_out, sent, joined, flat,
 ):
     gather_x(joined, own, (one, two, three))
@@ -422,6 +436,7 @@
     sent[...] = y_rows[...]
     sent[0:1, :] = first
     sent[1:2, :] = end
+    sent[5:6, :] = y_high[...]
 
 
 def second_x(
@@ -458,20 +473,14 @@
     out[...] = flat[...].T
 
 
-def call(body, shapes, args, scratch=(), scalars=(), near=True):
-    args = [
-        x if n in scalars else pltpu.with_memory_space_constraint(x, pltpu.VMEM)
-        for n, x in enumerate(args)
-    ]
+def call(body, shapes, args, scratch=(), fetched=True, near=True):
+    if fetched:
+        args = [pltpu.with_memory_space_constraint(x, pltpu.VMEM) for x in args]
     made = pltpu.VMEM if near else jax.ShapeDtypeStruct
-    specs = [
-        pl.BlockSpec(memory_space=pltpu.SMEM if n in scalars else pltpu.VMEM)
-        for n in range(len(args))
-    ]
     return pl.pallas_call(
         body,
         out_shape=[made((rows, LANES), jnp.float32) for rows in shapes],
-        in_specs=specs,
+        in_specs=[pl.BlockSpec(memory_space=pltpu.VMEM)] * len(args),
         out_specs=[pl.BlockSpec(memory_space=pltpu.VMEM)] * len(shapes),
         scratch_shapes=[pltpu.VMEM((rows, LANES), jnp.float32) for rows in scratch],
         name=body.__name__,
@@ -480,7 +489,7 @@
 
 def share_x(sent):
     return [
-        lax.ppermute(sent, "gx", [(i, (i + by) % COUNT_X) for i in range(COUNT_X)])
+        lax.ppermute(sent, "gx", [(i, i ^ by) for i in range(COUNT_X)])
         for by in range(1, COUNT_X)
     ]
 
@@ -493,30 +502,41 @@
     )
 
 
+def outside_pairs():
+    pairs = []
+    for x in range(COUNT_X):
+        for y in range(COUNT_Y):
+            if y in (0, COUNT_Y - 1):
+                to = ((x ^ 1), y)
+            else:
+                to = (x, y + 1 if y % 2 else y - 1)
+            pairs.append((x * COUNT_Y + y, to[0] * COUNT_Y + to[1]))
+    return pairs
+
+
 def local(starting_sag, warmth_celsius_field, junction_charge_store, load_amperes, source_patch_bits):
     v, warm, cap, load = starting_sag, warmth_celsius_field, junction_charge_store, load_amperes
-    v_t, warm_t, inside, outside = call(prepare, (ROWS, ROWS, 2, 2), (v, warm))
+    v_t, warm_t, outside = call(prepare, (ROWS, ROWS, 2), (v, warm), fetched=False)
+    outside = lax.ppermute(outside, ("gx", "gy"), outside_pairs())
+    coefs = SUB * LOCAL_COEFS
+    x_ref, x_rows, cap_t, y_edges, y_pad, inside = call(
+        factor_lines_x,
+        (coefs, SUB, ROWS, ROWS, SUB, 2),
+        (cap, warm, v_t, warm_t, source_patch_bits),
+    )
     inside = lax.ppermute(inside, "gy", [(i, i ^ 1) for i in range(COUNT_Y)])
-    pairs = [(i, (i + 1) % COUNT_Y if i % 2 else (i - 1) % COUNT_Y) for i in range(COUNT_Y)]
-    outside = lax.ppermute(outside, "gy", pairs)
-    coefs = SUB * LOCAL_COEFS
-    x_ref, y_ref, cap_t, x_rows, y_rows, y_edges, y_pad = call(
-        coefficients,
-        (coefs, coefs, ROWS, SUB, SUB, ROWS, SUB),
-        (cap, warm, warm_t, source_patch_bits),
-        scalars=(3,),
-    )
-    s, f, sent, y_rows = call(
+    y_ref, y_rows = call(factor_lines_y, (coefs, SUB), (cap_t, y_edges, y_pad))
+    s, f, sent, y_high = call(
         begin,
-        (ROWS, ROWS, SUB, SUB),
-        (v_t, warm_t, cap_t, load, inside, outside, y_edges, y_pad, y_rows, x_ref, x_rows),
+        (ROWS, ROWS, SUB, 1),
+        (v_t, warm_t, cap_t, load, inside, outside, y_edges, y_pad, x_ref, x_rows),
         scratch=(ROWS,),
     )
     joined = COUNT_X * SUB
     x_join, s, f, sent = call(
         first_x,
         (SUB * X_COEFS, ROWS, ROWS, SUB),
-        (sent, *share_x(sent), cap, load, s, f, x_ref, y_ref, y_rows),
+        (sent, *share_x(sent), cap, load, s, f, x_ref, y_ref, y_rows, y_high),
         scratch=(joined, ROWS),
     )
     y_join, s, f, sent = call(

time: 51.6 us -> 48.6 us (0.942)
  local copies, waits for them, and re-layouts: 1.75 us -> 0.04 us
  waiting for transfers between devices: 6.93 us -> 5.7 us
  blocking collectives: 30.9 us -> 29.7 us
  starting transfers between devices: 8.78 us -> 9.81 us
    ppermute x7, starting transfers between devices: 7.28 us -> 9.43 us  [the longest x6 6.66 us: share_x(): lax.ppermute(sent, 'gx', [(i, i ^ by) for i in range(COUNT_X)])]
    unnamed x8, local copies, waits for them, and re-layouts: 1.72 us -> 0.02 us
    ppermute x7, waiting for transfers between devices: 6.93 us -> 5.54 us  [the longest x6 4.87 us: share_x(): lax.ppermute(sent, 'gx', [(i, i ^ by) for i in range(COUNT_X)])]
    all_to_all x2, blocking collectives: 30.9 us -> 29.7 us  [share_y(): lax.all_to_all(copies, 'gy', split_axis=0, concat_axis=0, tiled=True)]
    ppermute x1, starting transfers between devices: 1.5 us -> 0.39 us  [local(): inside = lax.ppermute(inside, 'gy', [(i, i ^ 1) for i in range(COUNT_Y)])]
    pallas_call x7 -> x8, Pallas kernels: 2.87 us -> 3.12 us  [call(): pl.pallas_call(body, out_shape=[made((rows, LANES), jnp.float32) for rows...]
  transfers between devices with their start and end apart: 8 -> 8, of which waited for: 6 -> 6; matrix products, arithmetic and copies ran while one was open for 0% -> 0% of each run, Pallas kernels for 2% -> 1%
where the time goes in v3:
time: 48.6 us; the launch traced here: 48.4 us
  blocking collectives  29.7 us (61%)
  starting transfers between devices  9.81 us (20%)
  waiting for transfers between devices  5.7 us (12%)
  Pallas kernels  3.12 us (6%)
    all_to_all x2, blocking collectives, share_y(): lax.all_to_all(copies, 'gy', split_axis=0, concat_axis=0, tiled=True)  29.7 us
    ppermute x6, starting transfers between devices, share_x(): lax.ppermute(sent, 'gx', [(i, i ^ by) for i in range(COUNT_X)])  6.66 us
    ppermute x6, waiting for transfers between devices, share_x(): lax.ppermute(sent, 'gx', [(i, i ^ by) for i in range(COUNT_X)])  4.87 us
    pallas_call x8, Pallas kernels, call(): pl.pallas_call(body, out_shape=[made((rows, LANES), jnp.float32) for rows...  3.12 us
    ppermute x1, starting transfers between devices, local(): outside = lax.ppermute(outside, ('gx', 'gy'), outside_pairs())  2.77 us
  transfers between devices with their start and end apart: 8, of which 6 were waited for; matrix products, arithmetic and copies ran while one was open for 0% of the time, Pallas kernels for 1%

profile of v3, /device:TPU:1, one launch (start us, length us, event | category | flops | bytes accessed | tf_op | source)
XLA Modules:
  0.0 48.4 jit_solution(3715583781514879764)
XLA Ops:
  0.0 0.0 copy-start.2
  0.0 1.0 %prepare.1 = (f32[128,128]{1,0:T(8,128)S(1)}, f32[128,128]{1,0:T(8,128)S(1)}, f32[2,128]{1,0:T(2,128)S(1)}) custom-call(f32[128,128]{1,0:T(8,128)} %v.1, f32[128,128]{1,0:T(8,128)} %warm.3), custom_call_target="tpu_custom_call" | custom-call | tf_op jit(solution)/shard_map/prepare/pallas_call | solution.py:480
  1.0 0.0 copy-start.3
  1.0 2.8 %collective-permute-start.1 = (f32[2,128]{1,0:T(2,128)S(1)}, f32[2,128]{1,0:T(2,128)S(1)}, u32[]{:S(2)}, u32[]{:S(2)}) collective-permute-start(f32[2,128]{1,0:T(2,128)S(1)} %get-tuple-element.34), channel_id=1, source_target_pairs={{0,32},{1,2},{2,1},{3,4},{4,3},{5,6},{6,5},{7,8},{8,7},{9,10},{10,... | collective-permute-start | bytes 3080 | tf_op jit(solution)/shard_map/ppermute | solution.py:520
  3.8 0.0 copy-done.2
  3.8 0.0 copy-done.1
  3.8 0.0 copy-done.3
  3.8 0.2 factor_lines_x.1
  4.0 0.4 collective-permute-start
  4.4 0.7 %collective-permute-done.1.outside = f32[2,128]{1,0:T(2,128)S(1)} collective-permute-done((f32[2,128]{1,0:T(2,128)S(1)}, f32[2,128]{1,0:T(2,128)S(1)}, u32[]{:S(2)}, u32[]{:S(2)}) %collective-permute-start.1) | collective-permute-done | bytes 1056 | tf_op jit(solution)/shard_map/ppermute | solution.py:520
  5.1 0.2 collective-permute-done.inside
  5.2 0.0 copy-done
  5.2 0.2 begin.1
  5.4 2.6 %collective-permute-start.4 = (f32[8,128]{1,0:T(8,128)S(1)}, f32[8,128]{1,0:T(8,128)S(1)}, u32[]{:S(2)}, u32[]{:S(2)}) collective-permute-start(f32[8,128]{1,0:T(8,128)S(1)} %get-tuple-element.39.own), channel_id=1, source_target_pairs={{0,96},{32,64},{64,32},{96,0},{1,97},{33,65},{65,33},{97,1},{2,98}... | collective-permute-start | bytes 12296 | tf_op jit(solution)/shard_map/ppermute | solution.py:492
  8.0 0.5 %collective-permute-start.3 = (f32[8,128]{1,0:T(8,128)S(1)}, f32[8,128]{1,0:T(8,128)S(1)}, u32[]{:S(2)}, u32[]{:S(2)}) collective-permute-start(f32[8,128]{1,0:T(8,128)S(1)} %get-tuple-element.39.own), channel_id=1, source_target_pairs={{0,64},{32,96},{64,0},{96,32},{1,65},{33,97},{65,1},{97,33},{2,66}... | collective-permute-start | bytes 12296 | tf_op jit(solution)/shard_map/ppermute | solution.py:492
  8.5 0.3 collective-permute-start.2
  8.7 0.1 factor_lines_y.1
  8.8 0.3 collective-permute-done.4.three
  9.2 2.8 %collective-permute-done.3.two = f32[8,128]{1,0:T(8,128)S(1)} collective-permute-done((f32[8,128]{1,0:T(8,128)S(1)}, f32[8,128]{1,0:T(8,128)S(1)}, u32[]{:S(2)}, u32[]{:S(2)}) %collective-permute-start.3) | collective-permute-done | bytes 4128 | tf_op jit(solution)/shard_map/ppermute | solution.py:492
  11.9 0.0 collective-permute-done.2.one
  11.9 0.3 first_x.1
  12.2 17.4 %all_to_all.10 = f32[32,8,128]{2,1,0:T(8,128)S(1)} all-to-all(f32[32,8,128]{2,1,0:T(8,128)S(1)} %broadcast_in_dim.4), channel_id=1, replica_groups=mesh['gx'=4,'gy'=32] {'gy'}, dimensions={0} | all-to-all | bytes 262144 | tf_op jit(solution)/shard_map/all_to_all | solution.py:500
  29.6 0.3 first_y.1
  29.9 1.2 %collective-permute-start.7 = (f32[2,128]{1,0:T(2,128)S(1)}, f32[2,128]{1,0:T(2,128)S(1)}, u32[]{:S(2)}, u32[]{:S(2)}) collective-permute-start(f32[2,128]{1,0:T(2,128)S(1)} %get-tuple-element.48.own), channel_id=1, source_target_pairs={{0,96},{32,64},{64,32},{96,0},{1,97},{33,65},{65,33},{97,1},{2,98}... | collective-permute-start | bytes 3080 | tf_op jit(solution)/shard_map/ppermute | solution.py:492
  31.1 0.7 %collective-permute-start.6 = (f32[2,128]{1,0:T(2,128)S(1)}, f32[2,128]{1,0:T(2,128)S(1)}, u32[]{:S(2)}, u32[]{:S(2)}) collective-permute-start(f32[2,128]{1,0:T(2,128)S(1)} %get-tuple-element.48.own), channel_id=1, source_target_pairs={{0,64},{32,96},{64,0},{96,32},{1,65},{33,97},{65,1},{97,33},{2,66}... | collective-permute-start | bytes 3080 | tf_op jit(solution)/shard_map/ppermute | solution.py:492
  31.8 1.4 %collective-permute-start.5 = (f32[2,128]{1,0:T(2,128)S(1)}, f32[2,128]{1,0:T(2,128)S(1)}, u32[]{:S(2)}, u32[]{:S(2)}) collective-permute-start(f32[2,128]{1,0:T(2,128)S(1)} %get-tuple-element.48.own), channel_id=1, source_target_pairs={{0,32},{32,0},{64,96},{96,64},{1,33},{33,1},{65,97},{97,65},{2,34}... | collective-permute-start | bytes 3080 | tf_op jit(solution)/shard_map/ppermute | solution.py:492
  33.2 0.4 collective-permute-done.7.three
  33.6 1.4 %collective-permute-done.6.two = f32[2,128]{1,0:T(2,128)S(1)} collective-permute-done((f32[2,128]{1,0:T(2,128)S(1)}, f32[2,128]{1,0:T(2,128)S(1)}, u32[]{:S(2)}, u32[]{:S(2)}) %collective-permute-start.6) | collective-permute-done | bytes 1056 | tf_op jit(solution)/shard_map/ppermute | solution.py:492
  35.0 0.0 collective-permute-done.5.one
  35.0 0.2 second_x.1
  35.3 12.3 %all_to_all.11 = f32[32,2,128]{2,1,0:T(2,128)S(1)} all-to-all(f32[32,2,128]{2,1,0:T(2,128)S(1)} %broadcast_in_dim.5), channel_id=1, replica_groups=mesh['gx'=4,'gy'=32] {'gy'}, dimensions={0} | all-to-all | bytes 65536 | tf_op jit(solution)/shard_map/all_to_all | solution.py:500
  47.6 0.8 %second_y.1 = f32[128,128]{1,0:T(8,128)} custom-call(f32[64,128]{1,0:T(8,128)S(1)} %bitcast.3, f32[128,128]{1,0:T(8,128)S(1)} %get-tuple-element.53.f_in, f32[432,128]{1,0:T(8,128)S(1)} %get-tuple-element.42.y_ref, f32[248,128]{1,0:T(8,128)S(1)} %get-tuple-element.54.y_join), custom_call_target="tpu_custom_call" | custom-call | tf_op jit(solution)/shard_map/second_y/pallas_call | solution.py:480
  (4 shorter events, 0.0 us)
Async XLA Ops:
  0.0 3.8 %copy-start.2 = (f32[128,128]{1,0:T(8,128)S(1)}, f32[128,128]{1,0:T(8,128)}, u32[]{:S(2)}) copy-start(f32[128,128]{1,0:T(8,128)} %warm.3) | copy-start | bytes 196612
  0.0 3.8 %copy-start.1 = (f32[128,128]{1,0:T(8,128)S(1)}, f32[128,128]{1,0:T(8,128)}, u32[]{:S(2)}) copy-start(f32[128,128]{1,0:T(8,128)} %cap.5) | copy-start | bytes 196612
  1.0 2.8 %copy-start.3 = (s32[4,4]{1,0:T(4,128)S(1)}, s32[4,4]{1,0:T(4,128)}, u32[]{:S(2)}) copy-start(s32[4,4]{1,0:T(4,128)} %flags.1) | copy-start | bytes 196
  1.0 4.0 %collective-permute-start.1 = (f32[2,128]{1,0:T(2,128)S(1)}, f32[2,128]{1,0:T(2,128)S(1)}, u32[]{:S(2)}, u32[]{:S(2)}) collective-permute-start(f32[2,128]{1,0:T(2,128)S(1)} %get-tuple-element.34), channel_id=1, source_target_pairs={{0,32},{1,2},{2,1},{3,4},{4,3},{5,6},{6,5},{7,8},{8,7},{9,10},{10,... | collective-permute-start | bytes 3080 | tf_op jit(solution)/shard_map/ppermute | solution.py:520
  3.8 1.4 %copy-start = (f32[2,128,128]{2,1,0:T(8,128)S(1)}, f32[2,128,128]{2,1,0:T(8,128)}, u32[]{:S(2)}) copy-start(f32[2,128,128]{2,1,0:T(8,128)} %load.7) | copy-start | bytes 393220
  4.0 1.2 %collective-permute-start = (f32[2,128]{1,0:T(2,128)S(1)}, f32[2,128]{1,0:T(2,128)S(1)}, u32[]{:S(2)}, u32[]{:S(2)}) collective-permute-start(f32[2,128]{1,0:T(2,128)S(1)} %get-tuple-element.33), channel_id=1, source_target_pairs={{0,1},{1,0},{2,3},{3,2},{4,5},{5,4},{6,7},{7,6},{8,9},{9,8},{10,11... | collective-permute-start | bytes 3080 | tf_op jit(solution)/shard_map/ppermute | solution.py:527
  5.4 3.7 %collective-permute-start.4 = (f32[8,128]{1,0:T(8,128)S(1)}, f32[8,128]{1,0:T(8,128)S(1)}, u32[]{:S(2)}, u32[]{:S(2)}) collective-permute-start(f32[8,128]{1,0:T(8,128)S(1)} %get-tuple-element.39.own), channel_id=1, source_target_pairs={{0,96},{32,64},{64,32},{96,0},{1,97},{33,65},{65,33},{97,1},{2,98}... | collective-permute-start | bytes 12296 | tf_op jit(solution)/shard_map/ppermute | solution.py:492
  8.0 4.0 %collective-permute-start.3 = (f32[8,128]{1,0:T(8,128)S(1)}, f32[8,128]{1,0:T(8,128)S(1)}, u32[]{:S(2)}, u32[]{:S(2)}) collective-permute-start(f32[8,128]{1,0:T(8,128)S(1)} %get-tuple-element.39.own), channel_id=1, source_target_pairs={{0,64},{32,96},{64,0},{96,32},{1,65},{33,97},{65,1},{97,33},{2,66}... | collective-permute-start | bytes 12296 | tf_op jit(solution)/shard_map/ppermute | solution.py:492
  8.5 3.4 %collective-permute-start.2 = (f32[8,128]{1,0:T(8,128)S(1)}, f32[8,128]{1,0:T(8,128)S(1)}, u32[]{:S(2)}, u32[]{:S(2)}) collective-permute-start(f32[8,128]{1,0:T(8,128)S(1)} %get-tuple-element.39.own), channel_id=1, source_target_pairs={{0,32},{32,0},{64,96},{96,64},{1,33},{33,1},{65,97},{97,65},{2,34}... | collective-permute-start | bytes 12296 | tf_op jit(solution)/shard_map/ppermute | solution.py:492
  29.9 3.7 %collective-permute-start.7 = (f32[2,128]{1,0:T(2,128)S(1)}, f32[2,128]{1,0:T(2,128)S(1)}, u32[]{:S(2)}, u32[]{:S(2)}) collective-permute-start(f32[2,128]{1,0:T(2,128)S(1)} %get-tuple-element.48.own), channel_id=1, source_target_pairs={{0,96},{32,64},{64,32},{96,0},{1,97},{33,65},{65,33},{97,1},{2,98}... | collective-permute-start | bytes 3080 | tf_op jit(solution)/shard_map/ppermute | solution.py:492
  31.1 3.9 %collective-permute-start.6 = (f32[2,128]{1,0:T(2,128)S(1)}, f32[2,128]{1,0:T(2,128)S(1)}, u32[]{:S(2)}, u32[]{:S(2)}) collective-permute-start(f32[2,128]{1,0:T(2,128)S(1)} %get-tuple-element.48.own), channel_id=1, source_target_pairs={{0,64},{32,96},{64,0},{96,32},{1,65},{33,97},{65,1},{97,33},{2,66}... | collective-permute-start | bytes 3080 | tf_op jit(solution)/shard_map/ppermute | solution.py:492
  31.8 3.2 %collective-permute-start.5 = (f32[2,128]{1,0:T(2,128)S(1)}, f32[2,128]{1,0:T(2,128)S(1)}, u32[]{:S(2)}, u32[]{:S(2)}) collective-permute-start(f32[2,128]{1,0:T(2,128)S(1)} %get-tuple-element.48.own), channel_id=1, source_target_pairs={{0,32},{32,0},{64,96},{96,64},{1,33},{33,1},{65,97},{97,65},{2,34}... | collective-permute-start | bytes 3080 | tf_op jit(solution)/shard_map/ppermute | solution.py:492

commit v4 on v3

--- a/solution.py
+++ b/solution.py
@@ -26,6 +26,7 @@
     + [(4, 0, 8), (12, 8, 15), (8, 0, 15)]
 )
 SPANS = (1, 2, 4)
+X_TURNS = (1, 3, 2)
 LOCAL_COEFS = 3 * (len(INNER) + 1 + len(SPANS))
 
 def path_order(nodes):
@@ -169,7 +170,7 @@
     count = own.shape[0]
     joined[pl.ds(pl.multiple_of(place * SUB, SUB), count), :] = own[...]
     for n, other in enumerate(others):
-        source = jnp.bitwise_xor(place, n + 1)
+        source = jnp.bitwise_xor(place, X_TURNS[n])
         joined[pl.ds(pl.multiple_of(source * SUB, SUB), count), :] = other[...]
 
 
@@ -490,7 +491,7 @@
 def share_x(sent):
     return [
         lax.ppermute(sent, "gx", [(i, i ^ by) for i in range(COUNT_X)])
-        for by in range(1, COUNT_X)
+        for by in X_TURNS
     ]
 
 

time: 48.6 us -> 48.4 us (level)
  no operation moved by 1% of the time
where the time goes in v4:
time: 48.4 us; the launch traced here: 48.2 us
  blocking collectives  29.4 us (61%)
  starting transfers between devices  9.56 us (20%)
  waiting for transfers between devices  5.97 us (12%)
  Pallas kernels  3.12 us (6%)
    all_to_all x2, blocking collectives, share_y(): lax.all_to_all(copies, 'gy', split_axis=0, concat_axis=0, tiled=True)  29.4 us
    ppermute x6, starting transfers between devices, share_x(): lax.ppermute(sent, 'gx', [(i, i ^ by) for i in range(COUNT_X)])  6.41 us
    ppermute x6, waiting for transfers between devices, share_x(): lax.ppermute(sent, 'gx', [(i, i ^ by) for i in range(COUNT_X)])  5.15 us
    pallas_call x8, Pallas kernels, call(): pl.pallas_call(body, out_shape=[made((rows, LANES), jnp.float32) for rows...  3.12 us
    ppermute x1, starting transfers between devices, local(): outside = lax.ppermute(outside, ('gx', 'gy'), outside_pairs())  2.77 us
  transfers between devices with their start and end apart: 8, of which 6 were waited for; matrix products, arithmetic and copies ran while one was open for 0% of the time, Pallas kernels for 1%

profile of v4, /device:TPU:1, one launch (start us, length us, event | category | flops | bytes accessed | tf_op | source)
XLA Modules:
  0.0 48.2 jit_solution(13901239374955789862)
XLA Ops:
  0.0 0.0 copy-start.2
  0.0 1.0 %prepare.1 = (f32[128,128]{1,0:T(8,128)S(1)}, f32[128,128]{1,0:T(8,128)S(1)}, f32[2,128]{1,0:T(2,128)S(1)}) custom-call(f32[128,128]{1,0:T(8,128)} %v.1, f32[128,128]{1,0:T(8,128)} %warm.3), custom_call_target="tpu_custom_call" | custom-call | tf_op jit(solution)/shard_map/prepare/pallas_call | solution.py:481
  1.0 0.0 copy-start.3
  1.0 2.8 %collective-permute-start.1 = (f32[2,128]{1,0:T(2,128)S(1)}, f32[2,128]{1,0:T(2,128)S(1)}, u32[]{:S(2)}, u32[]{:S(2)}) collective-permute-start(f32[2,128]{1,0:T(2,128)S(1)} %get-tuple-element.34), channel_id=1, source_target_pairs={{0,32},{1,2},{2,1},{3,4},{4,3},{5,6},{6,5},{7,8},{8,7},{9,10},{10,... | collective-permute-start | bytes 3080 | tf_op jit(solution)/shard_map/ppermute | solution.py:521
  3.8 0.0 copy-done.2
  3.8 0.0 copy-done.1
  3.8 0.0 copy-done.3
  3.8 0.2 factor_lines_x.1
  4.0 0.4 collective-permute-start
  4.4 0.7 %collective-permute-done.1.outside = f32[2,128]{1,0:T(2,128)S(1)} collective-permute-done((f32[2,128]{1,0:T(2,128)S(1)}, f32[2,128]{1,0:T(2,128)S(1)}, u32[]{:S(2)}, u32[]{:S(2)}) %collective-permute-start.1) | collective-permute-done | bytes 1056 | tf_op jit(solution)/shard_map/ppermute | solution.py:521
  5.1 0.2 collective-permute-done.inside
  5.2 0.0 copy-done
  5.2 0.2 begin.1
  5.4 2.8 %collective-permute-start.4 = (f32[8,128]{1,0:T(8,128)S(1)}, f32[8,128]{1,0:T(8,128)S(1)}, u32[]{:S(2)}, u32[]{:S(2)}) collective-permute-start(f32[8,128]{1,0:T(8,128)S(1)} %get-tuple-element.39.own), channel_id=1, source_target_pairs={{0,64},{32,96},{64,0},{96,32},{1,65},{33,97},{65,1},{97,33},{2,66}... | collective-permute-start | bytes 12296 | tf_op jit(solution)/shard_map/ppermute | solution.py:493
  8.2 0.9 %collective-permute-start.3 = (f32[8,128]{1,0:T(8,128)S(1)}, f32[8,128]{1,0:T(8,128)S(1)}, u32[]{:S(2)}, u32[]{:S(2)}) collective-permute-start(f32[8,128]{1,0:T(8,128)S(1)} %get-tuple-element.39.own), channel_id=1, source_target_pairs={{0,96},{32,64},{64,32},{96,0},{1,97},{33,65},{65,33},{97,1},{2,98}... | collective-permute-start | bytes 12296 | tf_op jit(solution)/shard_map/ppermute | solution.py:493
  9.1 0.0 collective-permute-start.2
  9.1 0.1 factor_lines_y.1
  9.2 0.3 collective-permute-done.4.three
  9.5 2.5 %collective-permute-done.3.two = f32[8,128]{1,0:T(8,128)S(1)} collective-permute-done((f32[8,128]{1,0:T(8,128)S(1)}, f32[8,128]{1,0:T(8,128)S(1)}, u32[]{:S(2)}, u32[]{:S(2)}) %collective-permute-start.3) | collective-permute-done | bytes 4128 | tf_op jit(solution)/shard_map/ppermute | solution.py:493
  11.9 0.0 collective-permute-done.2.one
  11.9 0.3 first_x.1
  12.2 17.4 %all_to_all.10 = f32[32,8,128]{2,1,0:T(8,128)S(1)} all-to-all(f32[32,8,128]{2,1,0:T(8,128)S(1)} %broadcast_in_dim.4), channel_id=1, replica_groups=mesh['gx'=4,'gy'=32] {'gy'}, dimensions={0} | all-to-all | bytes 262144 | tf_op jit(solution)/shard_map/all_to_all | solution.py:501
  29.6 0.3 first_y.1
  29.9 1.3 %collective-permute-start.7 = (f32[2,128]{1,0:T(2,128)S(1)}, f32[2,128]{1,0:T(2,128)S(1)}, u32[]{:S(2)}, u32[]{:S(2)}) collective-permute-start(f32[2,128]{1,0:T(2,128)S(1)} %get-tuple-element.48.own), channel_id=1, source_target_pairs={{0,64},{32,96},{64,0},{96,32},{1,65},{33,97},{65,1},{97,33},{2,66}... | collective-permute-start | bytes 3080 | tf_op jit(solution)/shard_map/ppermute | solution.py:493
  31.1 0.9 %collective-permute-start.6 = (f32[2,128]{1,0:T(2,128)S(1)}, f32[2,128]{1,0:T(2,128)S(1)}, u32[]{:S(2)}, u32[]{:S(2)}) collective-permute-start(f32[2,128]{1,0:T(2,128)S(1)} %get-tuple-element.48.own), channel_id=1, source_target_pairs={{0,96},{32,64},{64,32},{96,0},{1,97},{33,65},{65,33},{97,1},{2,98}... | collective-permute-start | bytes 3080 | tf_op jit(solution)/shard_map/ppermute | solution.py:493
  32.0 0.6 %collective-permute-start.5 = (f32[2,128]{1,0:T(2,128)S(1)}, f32[2,128]{1,0:T(2,128)S(1)}, u32[]{:S(2)}, u32[]{:S(2)}) collective-permute-start(f32[2,128]{1,0:T(2,128)S(1)} %get-tuple-element.48.own), channel_id=1, source_target_pairs={{0,32},{32,0},{64,96},{96,64},{1,33},{33,1},{65,97},{97,65},{2,34}... | collective-permute-start | bytes 3080 | tf_op jit(solution)/shard_map/ppermute | solution.py:493
  32.6 1.3 %collective-permute-done.7.three = f32[2,128]{1,0:T(2,128)S(1)} collective-permute-done((f32[2,128]{1,0:T(2,128)S(1)}, f32[2,128]{1,0:T(2,128)S(1)}, u32[]{:S(2)}, u32[]{:S(2)}) %collective-permute-start.7) | collective-permute-done | bytes 1056 | tf_op jit(solution)/shard_map/ppermute | solution.py:493
  33.9 1.2 %collective-permute-done.6.two = f32[2,128]{1,0:T(2,128)S(1)} collective-permute-done((f32[2,128]{1,0:T(2,128)S(1)}, f32[2,128]{1,0:T(2,128)S(1)}, u32[]{:S(2)}, u32[]{:S(2)}) %collective-permute-start.6) | collective-permute-done | bytes 1056 | tf_op jit(solution)/shard_map/ppermute | solution.py:493
  35.0 0.0 collective-permute-done.5.one
  35.0 0.2 second_x.1
  35.3 12.1 %all_to_all.11 = f32[32,2,128]{2,1,0:T(2,128)S(1)} all-to-all(f32[32,2,128]{2,1,0:T(2,128)S(1)} %broadcast_in_dim.5), channel_id=1, replica_groups=mesh['gx'=4,'gy'=32] {'gy'}, dimensions={0} | all-to-all | bytes 65536 | tf_op jit(solution)/shard_map/all_to_all | solution.py:501
  47.3 0.8 %second_y.1 = f32[128,128]{1,0:T(8,128)} custom-call(f32[64,128]{1,0:T(8,128)S(1)} %bitcast.3, f32[128,128]{1,0:T(8,128)S(1)} %get-tuple-element.53.f_in, f32[432,128]{1,0:T(8,128)S(1)} %get-tuple-element.42.y_ref, f32[248,128]{1,0:T(8,128)S(1)} %get-tuple-element.54.y_join), custom_call_target="tpu_custom_call" | custom-call | tf_op jit(solution)/shard_map/second_y/pallas_call | solution.py:481
  (4 shorter events, 0.0 us)
Async XLA Ops:
  0.0 3.8 %copy-start.2 = (f32[128,128]{1,0:T(8,128)S(1)}, f32[128,128]{1,0:T(8,128)}, u32[]{:S(2)}) copy-start(f32[128,128]{1,0:T(8,128)} %warm.3) | copy-start | bytes 196612
  0.0 3.8 %copy-start.1 = (f32[128,128]{1,0:T(8,128)S(1)}, f32[128,128]{1,0:T(8,128)}, u32[]{:S(2)}) copy-start(f32[128,128]{1,0:T(8,128)} %cap.5) | copy-start | bytes 196612
  1.0 2.8 %copy-start.3 = (s32[4,4]{1,0:T(4,128)S(1)}, s32[4,4]{1,0:T(4,128)}, u32[]{:S(2)}) copy-start(s32[4,4]{1,0:T(4,128)} %flags.1) | copy-start | bytes 196
  1.0 4.0 %collective-permute-start.1 = (f32[2,128]{1,0:T(2,128)S(1)}, f32[2,128]{1,0:T(2,128)S(1)}, u32[]{:S(2)}, u32[]{:S(2)}) collective-permute-start(f32[2,128]{1,0:T(2,128)S(1)} %get-tuple-element.34), channel_id=1, source_target_pairs={{0,32},{1,2},{2,1},{3,4},{4,3},{5,6},{6,5},{7,8},{8,7},{9,10},{10,... | collective-permute-start | bytes 3080 | tf_op jit(solution)/shard_map/ppermute | solution.py:521
  3.8 1.4 %copy-start = (f32[2,128,128]{2,1,0:T(8,128)S(1)}, f32[2,128,128]{2,1,0:T(8,128)}, u32[]{:S(2)}) copy-start(f32[2,128,128]{2,1,0:T(8,128)} %load.7) | copy-start | bytes 393220
  4.0 1.2 %collective-permute-start = (f32[2,128]{1,0:T(2,128)S(1)}, f32[2,128]{1,0:T(2,128)S(1)}, u32[]{:S(2)}, u32[]{:S(2)}) collective-permute-start(f32[2,128]{1,0:T(2,128)S(1)} %get-tuple-element.33), channel_id=1, source_target_pairs={{0,1},{1,0},{2,3},{3,2},{4,5},{5,4},{6,7},{7,6},{8,9},{9,8},{10,11... | collective-permute-start | bytes 3080 | tf_op jit(solution)/shard_map/ppermute | solution.py:528
  5.4 4.0 %collective-permute-start.4 = (f32[8,128]{1,0:T(8,128)S(1)}, f32[8,128]{1,0:T(8,128)S(1)}, u32[]{:S(2)}, u32[]{:S(2)}) collective-permute-start(f32[8,128]{1,0:T(8,128)S(1)} %get-tuple-element.39.own), channel_id=1, source_target_pairs={{0,64},{32,96},{64,0},{96,32},{1,65},{33,97},{65,1},{97,33},{2,66}... | collective-permute-start | bytes 12296 | tf_op jit(solution)/shard_map/ppermute | solution.py:493
  8.2 3.7 %collective-permute-start.3 = (f32[8,128]{1,0:T(8,128)S(1)}, f32[8,128]{1,0:T(8,128)S(1)}, u32[]{:S(2)}, u32[]{:S(2)}) collective-permute-start(f32[8,128]{1,0:T(8,128)S(1)} %get-tuple-element.39.own), channel_id=1, source_target_pairs={{0,96},{32,64},{64,32},{96,0},{1,97},{33,65},{65,33},{97,1},{2,98}... | collective-permute-start | bytes 12296 | tf_op jit(solution)/shard_map/ppermute | solution.py:493
  9.1 2.8 %collective-permute-start.2 = (f32[8,128]{1,0:T(8,128)S(1)}, f32[8,128]{1,0:T(8,128)S(1)}, u32[]{:S(2)}, u32[]{:S(2)}) collective-permute-start(f32[8,128]{1,0:T(8,128)S(1)} %get-tuple-element.39.own), channel_id=1, source_target_pairs={{0,32},{32,0},{64,96},{96,64},{1,33},{33,1},{65,97},{97,65},{2,34}... | collective-permute-start | bytes 12296 | tf_op jit(solution)/shard_map/ppermute | solution.py:493
  29.9 4.0 %collective-permute-start.7 = (f32[2,128]{1,0:T(2,128)S(1)}, f32[2,128]{1,0:T(2,128)S(1)}, u32[]{:S(2)}, u32[]{:S(2)}) collective-permute-start(f32[2,128]{1,0:T(2,128)S(1)} %get-tuple-element.48.own), channel_id=1, source_target_pairs={{0,64},{32,96},{64,0},{96,32},{1,65},{33,97},{65,1},{97,33},{2,66}... | collective-permute-start | bytes 3080 | tf_op jit(solution)/shard_map/ppermute | solution.py:493
  31.1 3.9 %collective-permute-start.6 = (f32[2,128]{1,0:T(2,128)S(1)}, f32[2,128]{1,0:T(2,128)S(1)}, u32[]{:S(2)}, u32[]{:S(2)}) collective-permute-start(f32[2,128]{1,0:T(2,128)S(1)} %get-tuple-element.48.own), channel_id=1, source_target_pairs={{0,96},{32,64},{64,32},{96,0},{1,97},{33,65},{65,33},{97,1},{2,98}... | collective-permute-start | bytes 3080 | tf_op jit(solution)/shard_map/ppermute | solution.py:493
  32.0 3.0 %collective-permute-start.5 = (f32[2,128]{1,0:T(2,128)S(1)}, f32[2,128]{1,0:T(2,128)S(1)}, u32[]{:S(2)}, u32[]{:S(2)}) collective-permute-start(f32[2,128]{1,0:T(2,128)S(1)} %get-tuple-element.48.own), channel_id=1, source_target_pairs={{0,32},{32,0},{64,96},{96,64},{1,33},{33,1},{65,97},{97,65},{2,34}... | collective-permute-start | bytes 3080 | tf_op jit(solution)/shard_map/ppermute | solution.py:493

commit v5 on v4

--- a/solution.py
+++ b/solution.py
@@ -42,6 +42,7 @@
 X_ORDER = path_order(list(range(2 * COUNT_X)))
 X_COEFS = 3 * len(X_ORDER)
 Y_ORDER = [(1, 0, 2), (3, 2, 4), (5, 4, 6), (7, 6, 8), (2, 0, 4), (6, 4, 8), (4, 0, 8)]
+Y_SENT = 6
 Y_COEFS = 3 * (len(Y_ORDER) + len(SPANS)) + 1
 
 
@@ -234,7 +235,7 @@
     sub = sublanes()
 
     def part(r, q):
-        return joined[pl.ds(SUB * r + q, SUB, stride=SUB * Y_DEPTH), :]
+        return joined[pl.ds(Y_SENT * r + q, SUB, stride=Y_SENT * Y_DEPTH), :]
 
     ground, edges = {}, {}
     for r in range(Y_DEPTH):
@@ -434,10 +435,9 @@
     first, end = across_x(
         own, one, two, three, cap, load, 0, s_in, f_in, x_ref, y_ref, x_join, s_out, f_out, joined, flat
     )
-    sent[...] = y_rows[...]
-    sent[0:1, :] = first
-    sent[1:2, :] = end
-    sent[5:6, :] = y_high[...]
+    rows = [first, end, y_rows[2:3, :], y_rows[3:4, :], y_rows[4:5, :], y_high[...]]
+    for n, row in enumerate(rows):
+        sent[:, n * LANES : (n + 1) * LANES] = row
 
 
 def second_x(
@@ -455,7 +455,7 @@
     joined, cap_t, load, s_in, f_in, y_ref, x_ref, y_join, s_out, f_out, sent, found, flat
 ):
     factor_y(y_join, joined)
-    first, end = solve_y(y_join, joined, SUB, found)
+    first, end = solve_y(y_join, joined, Y_SENT, found)
     drop = backward_local(y_ref, load_regs(f_in), first, end)
     caps, source = load_lines(cap_t), load_regs(s_in)
     store_lines(flat, [2.0 * caps[r] * drop[r] - source[r] for r in range(DEPTH)])
@@ -480,7 +480,9 @@
     made = pltpu.VMEM if near else jax.ShapeDtypeStruct
     return pl.pallas_call(
         body,
-        out_shape=[made((rows, LANES), jnp.float32) for rows in shapes],
+        out_shape=[
+            made(rows if isinstance(rows, tuple) else (rows, LANES), jnp.float32) for rows in shapes
+        ],
         in_specs=[pl.BlockSpec(memory_space=pltpu.VMEM)] * len(args),
         out_specs=[pl.BlockSpec(memory_space=pltpu.VMEM)] * len(shapes),
         scratch_shapes=[pltpu.VMEM((rows, LANES), jnp.float32) for rows in scratch],
@@ -496,8 +498,8 @@
 
 
 def share_y(sent):
-    rows = sent.shape[0]
-    copies = jnp.broadcast_to(sent[None], (COUNT_Y, rows, LANES))
+    rows = sent.size // LANES
+    copies = jnp.broadcast_to(sent[None], (COUNT_Y, *sent.shape))
     return lax.all_to_all(copies, "gy", split_axis=0, concat_axis=0, tiled=True).reshape(
         COUNT_Y * rows, LANES
     )
@@ -536,7 +538,7 @@
     joined = COUNT_X * SUB
     x_join, s, f, sent = call(
         first_x,
-        (SUB * X_COEFS, ROWS, ROWS, SUB),
+        (SUB * X_COEFS, ROWS, ROWS, (1, Y_SENT * LANES)),
         (sent, *share_x(sent), cap, load, s, f, x_ref, y_ref, y_rows, y_high),
         scratch=(joined, ROWS),
     )

time: 48.4 us -> 48.2 us (level)
  no operation moved by 1% of the time
where the time goes in v5:
time: 48.2 us; the launch traced here: 47.9 us
  blocking collectives  29.1 us (60%)
  starting transfers between devices  9.56 us (20%)
  waiting for transfers between devices  5.96 us (12%)
  Pallas kernels  3.11 us (6%)
    all_to_all x2, blocking collectives, share_y(): lax.all_to_all(copies, 'gy', split_axis=0, concat_axis=0, tiled=True)  29.1 us
    ppermute x6, starting transfers between devices, share_x(): lax.ppermute(sent, 'gx', [(i, i ^ by) for i in range(COUNT_X)])  6.41 us
    ppermute x6, waiting for transfers between devices, share_x(): lax.ppermute(sent, 'gx', [(i, i ^ by) for i in range(COUNT_X)])  5.13 us
    pallas_call x8, Pallas kernels, call(): pl.pallas_call(body, out_shape=[made(rows if isinstance(rows, tuple) else...  3.11 us
    ppermute x1, starting transfers between devices, local(): outside = lax.ppermute(outside, ('gx', 'gy'), outside_pairs())  2.77 us
  transfers between devices with their start and end apart: 8, of which 6 were waited for; matrix products, arithmetic and copies ran while one was open for 0% of the time, Pallas kernels for 1%

profile of v5, /device:TPU:1, one launch (start us, length us, event | category | flops | bytes accessed | tf_op | source)
XLA Modules:
  0.0 47.9 jit_solution(9941220349764121716)
XLA Ops:
  0.0 1.0 %prepare.1 = (f32[128,128]{1,0:T(8,128)S(1)}, f32[128,128]{1,0:T(8,128)S(1)}, f32[2,128]{1,0:T(2,128)S(1)}) custom-call(f32[128,128]{1,0:T(8,128)} %v.1, f32[128,128]{1,0:T(8,128)} %warm.3), custom_call_target="tpu_custom_call" | custom-call | tf_op jit(solution)/shard_map/prepare/pallas_call | solution.py:481
  1.0 0.0 copy-start.3
  1.0 2.8 %collective-permute-start.1 = (f32[2,128]{1,0:T(2,128)S(1)}, f32[2,128]{1,0:T(2,128)S(1)}, u32[]{:S(2)}, u32[]{:S(2)}) collective-permute-start(f32[2,128]{1,0:T(2,128)S(1)} %get-tuple-element.34), channel_id=1, source_target_pairs={{0,32},{1,2},{2,1},{3,4},{4,3},{5,6},{6,5},{7,8},{8,7},{9,10},{10,... | collective-permute-start | bytes 3080 | tf_op jit(solution)/shard_map/ppermute | solution.py:523
  3.8 0.0 copy-done.2
  3.8 0.0 copy-done.1
  3.8 0.0 copy-done.3
  3.8 0.2 factor_lines_x.1
  4.0 0.4 collective-permute-start
  4.4 0.7 %collective-permute-done.1.outside = f32[2,128]{1,0:T(2,128)S(1)} collective-permute-done((f32[2,128]{1,0:T(2,128)S(1)}, f32[2,128]{1,0:T(2,128)S(1)}, u32[]{:S(2)}, u32[]{:S(2)}) %collective-permute-start.1) | collective-permute-done | bytes 1056 | tf_op jit(solution)/shard_map/ppermute | solution.py:523
  5.1 0.2 collective-permute-done.inside
  5.2 0.0 copy-done
  5.2 0.2 begin.1
  5.4 2.8 %collective-permute-start.4 = (f32[8,128]{1,0:T(8,128)S(1)}, f32[8,128]{1,0:T(8,128)S(1)}, u32[]{:S(2)}, u32[]{:S(2)}) collective-permute-start(f32[8,128]{1,0:T(8,128)S(1)} %get-tuple-element.39.own), channel_id=1, source_target_pairs={{0,64},{32,96},{64,0},{96,32},{1,65},{33,97},{65,1},{97,33},{2,66}... | collective-permute-start | bytes 12296 | tf_op jit(solution)/shard_map/ppermute | solution.py:495
  8.2 0.9 %collective-permute-start.3 = (f32[8,128]{1,0:T(8,128)S(1)}, f32[8,128]{1,0:T(8,128)S(1)}, u32[]{:S(2)}, u32[]{:S(2)}) collective-permute-start(f32[8,128]{1,0:T(8,128)S(1)} %get-tuple-element.39.own), channel_id=1, source_target_pairs={{0,96},{32,64},{64,32},{96,0},{1,97},{33,65},{65,33},{97,1},{2,98}... | collective-permute-start | bytes 12296 | tf_op jit(solution)/shard_map/ppermute | solution.py:495
  9.1 0.0 collective-permute-start.2
  9.1 0.1 factor_lines_y.1
  9.2 0.3 collective-permute-done.4.three
  9.5 2.5 %collective-permute-done.3.two = f32[8,128]{1,0:T(8,128)S(1)} collective-permute-done((f32[8,128]{1,0:T(8,128)S(1)}, f32[8,128]{1,0:T(8,128)S(1)}, u32[]{:S(2)}, u32[]{:S(2)}) %collective-permute-start.3) | collective-permute-done | bytes 4128 | tf_op jit(solution)/shard_map/ppermute | solution.py:495
  11.9 0.0 collective-permute-done.2.one
  11.9 0.3 first_x.1
  12.2 0.1 broadcast_in_dim.7
  12.3 17.1 %all_to_all.10 = f32[32,1,768]{2,1,0:T(1,128)S(1)} all-to-all(f32[32,1,768]{2,1,0:T(1,128)S(1)} %broadcast_in_dim.7), channel_id=1, replica_groups=mesh['gx'=4,'gy'=32] {'gy'}, dimensions={0} | all-to-all | bytes 196608 | tf_op jit(solution)/shard_map/all_to_all | solution.py:503
  29.4 0.3 first_y.1
  29.7 1.3 %collective-permute-start.7 = (f32[2,128]{1,0:T(2,128)S(1)}, f32[2,128]{1,0:T(2,128)S(1)}, u32[]{:S(2)}, u32[]{:S(2)}) collective-permute-start(f32[2,128]{1,0:T(2,128)S(1)} %get-tuple-element.48.own), channel_id=1, source_target_pairs={{0,64},{32,96},{64,0},{96,32},{1,65},{33,97},{65,1},{97,33},{2,66}... | collective-permute-start | bytes 3080 | tf_op jit(solution)/shard_map/ppermute | solution.py:495
  30.9 0.9 %collective-permute-start.6 = (f32[2,128]{1,0:T(2,128)S(1)}, f32[2,128]{1,0:T(2,128)S(1)}, u32[]{:S(2)}, u32[]{:S(2)}) collective-permute-start(f32[2,128]{1,0:T(2,128)S(1)} %get-tuple-element.48.own), channel_id=1, source_target_pairs={{0,96},{32,64},{64,32},{96,0},{1,97},{33,65},{65,33},{97,1},{2,98}... | collective-permute-start | bytes 3080 | tf_op jit(solution)/shard_map/ppermute | solution.py:495
  31.8 0.6 %collective-permute-start.5 = (f32[2,128]{1,0:T(2,128)S(1)}, f32[2,128]{1,0:T(2,128)S(1)}, u32[]{:S(2)}, u32[]{:S(2)}) collective-permute-start(f32[2,128]{1,0:T(2,128)S(1)} %get-tuple-element.48.own), channel_id=1, source_target_pairs={{0,32},{32,0},{64,96},{96,64},{1,33},{33,1},{65,97},{97,65},{2,34}... | collective-permute-start | bytes 3080 | tf_op jit(solution)/shard_map/ppermute | solution.py:495
  32.4 1.3 %collective-permute-done.7.three = f32[2,128]{1,0:T(2,128)S(1)} collective-permute-done((f32[2,128]{1,0:T(2,128)S(1)}, f32[2,128]{1,0:T(2,128)S(1)}, u32[]{:S(2)}, u32[]{:S(2)}) %collective-permute-start.7) | collective-permute-done | bytes 1056 | tf_op jit(solution)/shard_map/ppermute | solution.py:495
  33.7 1.1 %collective-permute-done.6.two = f32[2,128]{1,0:T(2,128)S(1)} collective-permute-done((f32[2,128]{1,0:T(2,128)S(1)}, f32[2,128]{1,0:T(2,128)S(1)}, u32[]{:S(2)}, u32[]{:S(2)}) %collective-permute-start.6) | collective-permute-done | bytes 1056 | tf_op jit(solution)/shard_map/ppermute | solution.py:495
  34.8 0.0 collective-permute-done.5.one
  34.8 0.2 second_x.1
  35.1 12.0 %all_to_all.11 = f32[32,2,128]{2,1,0:T(2,128)S(1)} all-to-all(f32[32,2,128]{2,1,0:T(2,128)S(1)} %broadcast_in_dim.16), channel_id=1, replica_groups=mesh['gx'=4,'gy'=32] {'gy'}, dimensions={0} | all-to-all | bytes 65536 | tf_op jit(solution)/shard_map/all_to_all | solution.py:503
  47.1 0.8 %second_y.1 = f32[128,128]{1,0:T(8,128)} custom-call(f32[64,128]{1,0:T(8,128)S(1)} %bitcast.3, f32[128,128]{1,0:T(8,128)S(1)} %get-tuple-element.53.f_in, f32[432,128]{1,0:T(8,128)S(1)} %get-tuple-element.42.y_ref, f32[248,128]{1,0:T(8,128)S(1)} %get-tuple-element.54.y_join), custom_call_target="tpu_custom_call" | custom-call | tf_op jit(solution)/shard_map/second_y/pallas_call | solution.py:481
  (5 shorter events, 0.0 us)
Async XLA Ops:
  0.0 3.8 %copy-start.2 = (f32[128,128]{1,0:T(8,128)S(1)}, f32[128,128]{1,0:T(8,128)}, u32[]{:S(2)}) copy-start(f32[128,128]{1,0:T(8,128)} %warm.3) | copy-start | bytes 196612
  0.0 3.8 %copy-start.1 = (f32[128,128]{1,0:T(8,128)S(1)}, f32[128,128]{1,0:T(8,128)}, u32[]{:S(2)}) copy-start(f32[128,128]{1,0:T(8,128)} %cap.5) | copy-start | bytes 196612
  1.0 2.8 %copy-start.3 = (s32[4,4]{1,0:T(4,128)S(1)}, s32[4,4]{1,0:T(4,128)}, u32[]{:S(2)}) copy-start(s32[4,4]{1,0:T(4,128)} %flags.1) | copy-start | bytes 196
  1.0 4.0 %collective-permute-start.1 = (f32[2,128]{1,0:T(2,128)S(1)}, f32[2,128]{1,0:T(2,128)S(1)}, u32[]{:S(2)}, u32[]{:S(2)}) collective-permute-start(f32[2,128]{1,0:T(2,128)S(1)} %get-tuple-element.34), channel_id=1, source_target_pairs={{0,32},{1,2},{2,1},{3,4},{4,3},{5,6},{6,5},{7,8},{8,7},{9,10},{10,... | collective-permute-start | bytes 3080 | tf_op jit(solution)/shard_map/ppermute | solution.py:523
  3.8 1.4 %copy-start = (f32[2,128,128]{2,1,0:T(8,128)S(1)}, f32[2,128,128]{2,1,0:T(8,128)}, u32[]{:S(2)}) copy-start(f32[2,128,128]{2,1,0:T(8,128)} %load.7) | copy-start | bytes 393220
  4.0 1.2 %collective-permute-start = (f32[2,128]{1,0:T(2,128)S(1)}, f32[2,128]{1,0:T(2,128)S(1)}, u32[]{:S(2)}, u32[]{:S(2)}) collective-permute-start(f32[2,128]{1,0:T(2,128)S(1)} %get-tuple-element.33), channel_id=1, source_target_pairs={{0,1},{1,0},{2,3},{3,2},{4,5},{5,4},{6,7},{7,6},{8,9},{9,8},{10,11... | collective-permute-start | bytes 3080 | tf_op jit(solution)/shard_map/ppermute | solution.py:530
  5.4 4.0 %collective-permute-start.4 = (f32[8,128]{1,0:T(8,128)S(1)}, f32[8,128]{1,0:T(8,128)S(1)}, u32[]{:S(2)}, u32[]{:S(2)}) collective-permute-start(f32[8,128]{1,0:T(8,128)S(1)} %get-tuple-element.39.own), channel_id=1, source_target_pairs={{0,64},{32,96},{64,0},{96,32},{1,65},{33,97},{65,1},{97,33},{2,66}... | collective-permute-start | bytes 12296 | tf_op jit(solution)/shard_map/ppermute | solution.py:495
  8.2 3.7 %collective-permute-start.3 = (f32[8,128]{1,0:T(8,128)S(1)}, f32[8,128]{1,0:T(8,128)S(1)}, u32[]{:S(2)}, u32[]{:S(2)}) collective-permute-start(f32[8,128]{1,0:T(8,128)S(1)} %get-tuple-element.39.own), channel_id=1, source_target_pairs={{0,96},{32,64},{64,32},{96,0},{1,97},{33,65},{65,33},{97,1},{2,98}... | collective-permute-start | bytes 12296 | tf_op jit(solution)/shard_map/ppermute | solution.py:495
  9.1 2.8 %collective-permute-start.2 = (f32[8,128]{1,0:T(8,128)S(1)}, f32[8,128]{1,0:T(8,128)S(1)}, u32[]{:S(2)}, u32[]{:S(2)}) collective-permute-start(f32[8,128]{1,0:T(8,128)S(1)} %get-tuple-element.39.own), channel_id=1, source_target_pairs={{0,32},{32,0},{64,96},{96,64},{1,33},{33,1},{65,97},{97,65},{2,34}... | collective-permute-start | bytes 12296 | tf_op jit(solution)/shard_map/ppermute | solution.py:495
  29.7 4.0 %collective-permute-start.7 = (f32[2,128]{1,0:T(2,128)S(1)}, f32[2,128]{1,0:T(2,128)S(1)}, u32[]{:S(2)}, u32[]{:S(2)}) collective-permute-start(f32[2,128]{1,0:T(2,128)S(1)} %get-tuple-element.48.own), channel_id=1, source_target_pairs={{0,64},{32,96},{64,0},{96,32},{1,65},{33,97},{65,1},{97,33},{2,66}... | collective-permute-start | bytes 3080 | tf_op jit(solution)/shard_map/ppermute | solution.py:495
  30.9 3.9 %collective-permute-start.6 = (f32[2,128]{1,0:T(2,128)S(1)}, f32[2,128]{1,0:T(2,128)S(1)}, u32[]{:S(2)}, u32[]{:S(2)}) collective-permute-start(f32[2,128]{1,0:T(2,128)S(1)} %get-tuple-element.48.own), channel_id=1, source_target_pairs={{0,96},{32,64},{64,32},{96,0},{1,97},{33,65},{65,33},{97,1},{2,98}... | collective-permute-start | bytes 3080 | tf_op jit(solution)/shard_map/ppermute | solution.py:495
  31.8 3.0 %collective-permute-start.5 = (f32[2,128]{1,0:T(2,128)S(1)}, f32[2,128]{1,0:T(2,128)S(1)}, u32[]{:S(2)}, u32[]{:S(2)}) collective-permute-start(f32[2,128]{1,0:T(2,128)S(1)} %get-tuple-element.48.own), channel_id=1, source_target_pairs={{0,32},{32,0},{64,96},{96,64},{1,33},{33,1},{65,97},{97,65},{2,34}... | collective-permute-start | bytes 3080 | tf_op jit(solution)/shard_map/ppermute | solution.py:495

commit v6 on v5

--- a/solution.py
+++ b/solution.py
@@ -41,8 +41,8 @@
 
 X_ORDER = path_order(list(range(2 * COUNT_X)))
 X_COEFS = 3 * len(X_ORDER)
-Y_ORDER = [(1, 0, 2), (3, 2, 4), (5, 4, 6), (7, 6, 8), (2, 0, 4), (6, 4, 8), (4, 0, 8)]
-Y_SENT = 6
+Y_ORDER = [(1, 0, 2), (3, 2, 4), (2, 0, 4)]
+Y_SENT = 5
 Y_COEFS = 3 * (len(Y_ORDER) + len(SPANS)) + 1
 
 
@@ -239,9 +239,10 @@
 
     ground, edges = {}, {}
     for r in range(Y_DEPTH):
-        ground[2 * r], ground[2 * r + 1] = part(r, 2), part(r, 3)
-        edges[(2 * r, 2 * r + 1)], edges[(2 * r + 1, 2 * r + 2)] = part(r, 4), part(r, 5)
-    last = 2 * Y_DEPTH
+        passed = part(r - 1, 3) if r > 0 else roll(part(Y_DEPTH - 1, 3), 1)
+        ground[r] = part(r, 2) + passed
+        edges[(r, r + 1)] = part(r, 4)
+    last = Y_DEPTH
     for k, (m, left, right) in enumerate(Y_ORDER):
         to_left, to_right = edges[(left, m)], edges[(m, right)]
         inverse = 1.0 / (to_left + to_right + ground[m])
@@ -266,13 +267,17 @@
     ref[pl.ds(SUB * (Y_COEFS - 1), SUB), :] = jnp.where(sub == 0, 1.0 / first, 0.0)
 
 
-def solve_y(ref, joined, stride, found):
-    sub = sublanes()
-    last = 2 * Y_DEPTH
-    f = [
-        joined[pl.ds(stride * (n // 2) + n % 2, SUB, stride=stride * Y_DEPTH), :]
-        for n in range(last)
-    ]
+def solve_y(ref, joined, stride, link, held, found):
+    sub = sublanes()
+    last = Y_DEPTH
+
+    def part(r, q):
+        return joined[pl.ds(stride * r + q, SUB, stride=stride * Y_DEPTH), :]
+
+    f = []
+    for r in range(Y_DEPTH):
+        passed = part(r - 1, 1) if r > 0 else roll(part(Y_DEPTH - 1, 1), 1)
+        f.append(part(r, 0) + passed)
     for k, (m, left, right) in enumerate(Y_ORDER):
         _, by_left, by_right = coef(ref, k)
         f[left] = f[left] + by_left * f[m]
@@ -297,8 +302,13 @@
         x[m] = inverse * f[m] + by_left * x[left] + by_right * x[right]
     store_regs(found, x[:last])
     place = lax.axis_index("gy")
-    at = lax.rem(place, Y_DEPTH) * (2 * SUB) + lax.div(place, Y_DEPTH)
-    return spread(found[pl.ds(at, 1), :]), spread(found[pl.ds(at + SUB, 1), :])
+    rows = []
+    for at in (place, lax.rem(place + 1, COUNT_Y)):
+        at = lax.rem(at, Y_DEPTH) * SUB + lax.div(at, Y_DEPTH)
+        rows.append(found[pl.ds(at, 1), :])
+    first, beyond = rows
+    end = link[0:1, :] * held[...] + link[1:2, :] * first + link[2:3, :] * beyond
+    return spread(first), spread(end)
 
 
 def put_rim(ref, v_t, warm_t, low):
@@ -428,34 +438,40 @@
 
 def first_x(
     own, one, two, three, cap, load, s_in, f_in, x_ref, y_ref, y_rows, y_high,
-    x_join, s_out, f_out, sent, joined, flat,
+    x_join, s_out, f_out, sent, link, held, joined, flat,
 ):
     gather_x(joined, own, (one, two, three))
     factor_x(x_join, joined)
     first, end = across_x(
         own, one, two, three, cap, load, 0, s_in, f_in, x_ref, y_ref, x_join, s_out, f_out, joined, flat
     )
-    rows = [first, end, y_rows[2:3, :], y_rows[3:4, :], y_rows[4:5, :], y_high[...]]
+    own, across, end_ground = y_rows[4:5, :], y_high[...], y_rows[3:4, :]
+    inverse = 1.0 / (own + across + end_ground)
+    by_left, by_right = own * inverse, across * inverse
+    put_rows(link, [inverse, by_left, by_right])
+    held[...] = end
+    rows = [first + by_left * end, by_right * end]
+    rows += [y_rows[2:3, :] + by_left * end_ground, by_right * end_ground, own * by_right]
     for n, row in enumerate(rows):
         sent[:, n * LANES : (n + 1) * LANES] = row
 
 
 def second_x(
-    own, one, two, three, cap, load, s_in, f_in, x_ref, y_ref, x_join, f_out, sent, joined, flat
+    own, one, two, three, cap, load, s_in, f_in, x_ref, y_ref, x_join, link, f_out, sent, held, joined, flat
 ):
     gather_x(joined, own, (one, two, three))
     first, end = across_x(
         own, one, two, three, cap, load, 1, s_in, f_in, x_ref, y_ref, x_join, None, f_out, joined, flat
     )
-    sent[0:1, :] = first
-    sent[1:2, :] = end
+    held[...] = end
+    put_rows(sent, [first + link[1:2, :] * end, link[2:3, :] * end])
 
 
 def first_y(
-    joined, cap_t, load, s_in, f_in, y_ref, x_ref, y_join, s_out, f_out, sent, found, flat
+    joined, cap_t, load, s_in, f_in, y_ref, x_ref, link, held, y_join, s_out, f_out, sent, found, flat
 ):
     factor_y(y_join, joined)
-    first, end = solve_y(y_join, joined, Y_SENT, found)
+    first, end = solve_y(y_join, joined, Y_SENT, link, held, found)
     drop = backward_local(y_ref, load_regs(f_in), first, end)
     caps, source = load_lines(cap_t), load_regs(s_in)
     store_lines(flat, [2.0 * caps[r] * drop[r] - source[r] for r in range(DEPTH)])
@@ -468,8 +484,8 @@
     sent[1:2, :] = end
 
 
-def second_y(joined, f_in, y_ref, y_join, out, found, flat):
-    first, end = solve_y(y_join, joined, 2, found)
+def second_y(joined, f_in, y_ref, y_join, link, held, out, found, flat):
+    first, end = solve_y(y_join, joined, 2, link, held, found)
     store_lines(flat, backward_local(y_ref, load_regs(f_in), first, end))
     out[...] = flat[...].T
 
@@ -536,29 +552,29 @@
         scratch=(ROWS,),
     )
     joined = COUNT_X * SUB
-    x_join, s, f, sent = call(
+    x_join, s, f, sent, link, held = call(
         first_x,
-        (SUB * X_COEFS, ROWS, ROWS, (1, Y_SENT * LANES)),
+        (SUB * X_COEFS, ROWS, ROWS, (1, Y_SENT * LANES), 3, 1),
         (sent, *share_x(sent), cap, load, s, f, x_ref, y_ref, y_rows, y_high),
         scratch=(joined, ROWS),
     )
     y_join, s, f, sent = call(
         first_y,
         (SUB * Y_COEFS, ROWS, ROWS, 2),
-        (share_y(sent), cap_t, load, s, f, y_ref, x_ref),
-        scratch=(2 * Y_DEPTH * SUB, ROWS),
-    )
-    f, sent = call(
+        (share_y(sent), cap_t, load, s, f, y_ref, x_ref, link, held),
+        scratch=(Y_DEPTH * SUB, ROWS),
+    )
+    f, sent, held = call(
         second_x,
-        (ROWS, 2),
-        (sent, *share_x(sent), cap, load, s, f, x_ref, y_ref, x_join),
+        (ROWS, 2, 1),
+        (sent, *share_x(sent), cap, load, s, f, x_ref, y_ref, x_join, link),
         scratch=(joined, ROWS),
     )
     (drop,) = call(
         second_y,
         (ROWS,),
-        (share_y(sent), f, y_ref, y_join),
-        scratch=(2 * Y_DEPTH * SUB, ROWS),
+        (share_y(sent), f, y_ref, y_join, link, held),
+        scratch=(Y_DEPTH * SUB, ROWS),
         near=False,
     )
     return drop

time: 48.2 us -> 48.1 us (level)
  no operation moved by 1% of the time
where the time goes in v6:
time: 48.1 us; the launch traced here: 47.9 us
  blocking collectives  29.1 us (60%)
  starting transfers between devices  9.56 us (20%)
  waiting for transfers between devices  5.96 us (12%)
  Pallas kernels  3.09 us (6%)
    all_to_all x2, blocking collectives, share_y(): lax.all_to_all(copies, 'gy', split_axis=0, concat_axis=0, tiled=True)  29.1 us
    ppermute x6, starting transfers between devices, share_x(): lax.ppermute(sent, 'gx', [(i, i ^ by) for i in range(COUNT_X)])  6.41 us
    ppermute x6, waiting for transfers between devices, share_x(): lax.ppermute(sent, 'gx', [(i, i ^ by) for i in range(COUNT_X)])  5.13 us
    pallas_call x8, Pallas kernels, call(): pl.pallas_call(body, out_shape=[made(rows if isinstance(rows, tuple) else...  3.09 us
    ppermute x1, starting transfers between devices, local(): outside = lax.ppermute(outside, ('gx', 'gy'), outside_pairs())  2.77 us
  transfers between devices with their start and end apart: 8, of which 6 were waited for; matrix products, arithmetic and copies ran while one was open for 0% of the time, Pallas kernels for 1%

profile of v6, /device:TPU:1, one launch (start us, length us, event | category | flops | bytes accessed | tf_op | source)
XLA Modules:
  0.0 47.9 jit_solution(16276947658600620544)
XLA Ops:
  0.0 0.0 copy-start.2
  0.0 1.0 %prepare.1 = (f32[128,128]{1,0:T(8,128)S(1)}, f32[128,128]{1,0:T(8,128)S(1)}, f32[2,128]{1,0:T(2,128)S(1)}) custom-call(f32[128,128]{1,0:T(8,128)} %v.1, f32[128,128]{1,0:T(8,128)} %warm.3), custom_call_target="tpu_custom_call" | custom-call | tf_op jit(solution)/shard_map/prepare/pallas_call | solution.py:497
  1.0 0.0 copy-start.3
  1.0 2.8 %collective-permute-start.1 = (f32[2,128]{1,0:T(2,128)S(1)}, f32[2,128]{1,0:T(2,128)S(1)}, u32[]{:S(2)}, u32[]{:S(2)}) collective-permute-start(f32[2,128]{1,0:T(2,128)S(1)} %get-tuple-element.37), channel_id=1, source_target_pairs={{0,32},{1,2},{2,1},{3,4},{4,3},{5,6},{6,5},{7,8},{8,7},{9,10},{10,... | collective-permute-start | bytes 3080 | tf_op jit(solution)/shard_map/ppermute | solution.py:539
  3.8 0.0 copy-done.2
  3.8 0.0 copy-done.1
  3.8 0.0 copy-done.3
  3.8 0.2 factor_lines_x.1
  4.0 0.4 collective-permute-start
  4.4 0.7 %collective-permute-done.1.outside = f32[2,128]{1,0:T(2,128)S(1)} collective-permute-done((f32[2,128]{1,0:T(2,128)S(1)}, f32[2,128]{1,0:T(2,128)S(1)}, u32[]{:S(2)}, u32[]{:S(2)}) %collective-permute-start.1) | collective-permute-done | bytes 1056 | tf_op jit(solution)/shard_map/ppermute | solution.py:539
  5.1 0.2 collective-permute-done.inside
  5.2 0.0 copy-done
  5.2 0.2 begin.1
  5.4 2.8 %collective-permute-start.4 = (f32[8,128]{1,0:T(8,128)S(1)}, f32[8,128]{1,0:T(8,128)S(1)}, u32[]{:S(2)}, u32[]{:S(2)}) collective-permute-start(f32[8,128]{1,0:T(8,128)S(1)} %get-tuple-element.42.own), channel_id=1, source_target_pairs={{0,64},{32,96},{64,0},{96,32},{1,65},{33,97},{65,1},{97,33},{2,66}... | collective-permute-start | bytes 12296 | tf_op jit(solution)/shard_map/ppermute | solution.py:511
  8.2 0.9 %collective-permute-start.3 = (f32[8,128]{1,0:T(8,128)S(1)}, f32[8,128]{1,0:T(8,128)S(1)}, u32[]{:S(2)}, u32[]{:S(2)}) collective-permute-start(f32[8,128]{1,0:T(8,128)S(1)} %get-tuple-element.42.own), channel_id=1, source_target_pairs={{0,96},{32,64},{64,32},{96,0},{1,97},{33,65},{65,33},{97,1},{2,98}... | collective-permute-start | bytes 12296 | tf_op jit(solution)/shard_map/ppermute | solution.py:511
  9.1 0.0 collective-permute-start.2
  9.1 0.1 factor_lines_y.1
  9.2 0.3 collective-permute-done.4.three
  9.5 2.5 %collective-permute-done.3.two = f32[8,128]{1,0:T(8,128)S(1)} collective-permute-done((f32[8,128]{1,0:T(8,128)S(1)}, f32[8,128]{1,0:T(8,128)S(1)}, u32[]{:S(2)}, u32[]{:S(2)}) %collective-permute-start.3) | collective-permute-done | bytes 4128 | tf_op jit(solution)/shard_map/ppermute | solution.py:511
  11.9 0.0 collective-permute-done.2.one
  11.9 0.3 first_x.1
  12.2 17.1 %all_to_all.10 = f32[32,1,640]{2,1,0:T(1,128)S(1)} all-to-all(f32[32,1,640]{2,1,0:T(1,128)S(1)} %broadcast_in_dim.7), channel_id=1, replica_groups=mesh['gx'=4,'gy'=32] {'gy'}, dimensions={0} | all-to-all | bytes 163840 | tf_op jit(solution)/shard_map/all_to_all | solution.py:519
  29.3 0.3 first_y.1
  29.6 1.3 %collective-permute-start.7 = (f32[2,128]{1,0:T(2,128)S(1)}, f32[2,128]{1,0:T(2,128)S(1)}, u32[]{:S(2)}, u32[]{:S(2)}) collective-permute-start(f32[2,128]{1,0:T(2,128)S(1)} %get-tuple-element.53.own), channel_id=1, source_target_pairs={{0,64},{32,96},{64,0},{96,32},{1,65},{33,97},{65,1},{97,33},{2,66}... | collective-permute-start | bytes 3080 | tf_op jit(solution)/shard_map/ppermute | solution.py:511
  30.9 0.9 %collective-permute-start.6 = (f32[2,128]{1,0:T(2,128)S(1)}, f32[2,128]{1,0:T(2,128)S(1)}, u32[]{:S(2)}, u32[]{:S(2)}) collective-permute-start(f32[2,128]{1,0:T(2,128)S(1)} %get-tuple-element.53.own), channel_id=1, source_target_pairs={{0,96},{32,64},{64,32},{96,0},{1,97},{33,65},{65,33},{97,1},{2,98}... | collective-permute-start | bytes 3080 | tf_op jit(solution)/shard_map/ppermute | solution.py:511
  31.7 0.6 %collective-permute-start.5 = (f32[2,128]{1,0:T(2,128)S(1)}, f32[2,128]{1,0:T(2,128)S(1)}, u32[]{:S(2)}, u32[]{:S(2)}) collective-permute-start(f32[2,128]{1,0:T(2,128)S(1)} %get-tuple-element.53.own), channel_id=1, source_target_pairs={{0,32},{32,0},{64,96},{96,64},{1,33},{33,1},{65,97},{97,65},{2,34}... | collective-permute-start | bytes 3080 | tf_op jit(solution)/shard_map/ppermute | solution.py:511
  32.3 1.3 %collective-permute-done.7.three = f32[2,128]{1,0:T(2,128)S(1)} collective-permute-done((f32[2,128]{1,0:T(2,128)S(1)}, f32[2,128]{1,0:T(2,128)S(1)}, u32[]{:S(2)}, u32[]{:S(2)}) %collective-permute-start.7) | collective-permute-done | bytes 1056 | tf_op jit(solution)/shard_map/ppermute | solution.py:511
  33.6 1.1 %collective-permute-done.6.two = f32[2,128]{1,0:T(2,128)S(1)} collective-permute-done((f32[2,128]{1,0:T(2,128)S(1)}, f32[2,128]{1,0:T(2,128)S(1)}, u32[]{:S(2)}, u32[]{:S(2)}) %collective-permute-start.6) | collective-permute-done | bytes 1056 | tf_op jit(solution)/shard_map/ppermute | solution.py:511
  34.8 0.0 collective-permute-done.5.one
  34.8 0.2 second_x.1
  35.0 12.0 %all_to_all.11 = f32[32,2,128]{2,1,0:T(2,128)S(1)} all-to-all(f32[32,2,128]{2,1,0:T(2,128)S(1)} %broadcast_in_dim.16), channel_id=1, replica_groups=mesh['gx'=4,'gy'=32] {'gy'}, dimensions={0} | all-to-all | bytes 65536 | tf_op jit(solution)/shard_map/all_to_all | solution.py:519
  47.0 0.8 %second_y.1 = f32[128,128]{1,0:T(8,128)} custom-call(f32[64,128]{1,0:T(8,128)S(1)} %bitcast.3, f32[128,128]{1,0:T(8,128)S(1)} %get-tuple-element.58.f_in, f32[432,128]{1,0:T(8,128)S(1)} %get-tuple-element.45.y_ref, f32[152,128]{1,0:T(8,128)S(1)} %get-tuple-element.59.y_join, f32[3,128]{1,0:T(4,128)S(1)} %get-tuple-element.51.link, ...), custom_call_target="tpu_custom_call" | custom-call | tf_op jit(solution)/shard_map/second_y/pallas_call | solution.py:497
  (5 shorter events, 0.1 us)
Async XLA Ops:
  0.0 3.8 %copy-start.2 = (f32[128,128]{1,0:T(8,128)S(1)}, f32[128,128]{1,0:T(8,128)}, u32[]{:S(2)}) copy-start(f32[128,128]{1,0:T(8,128)} %warm.3) | copy-start | bytes 196612
  0.0 3.8 %copy-start.1 = (f32[128,128]{1,0:T(8,128)S(1)}, f32[128,128]{1,0:T(8,128)}, u32[]{:S(2)}) copy-start(f32[128,128]{1,0:T(8,128)} %cap.5) | copy-start | bytes 196612
  1.0 2.8 %copy-start.3 = (s32[4,4]{1,0:T(4,128)S(1)}, s32[4,4]{1,0:T(4,128)}, u32[]{:S(2)}) copy-start(s32[4,4]{1,0:T(4,128)} %flags.1) | copy-start | bytes 196
  1.0 4.0 %collective-permute-start.1 = (f32[2,128]{1,0:T(2,128)S(1)}, f32[2,128]{1,0:T(2,128)S(1)}, u32[]{:S(2)}, u32[]{:S(2)}) collective-permute-start(f32[2,128]{1,0:T(2,128)S(1)} %get-tuple-element.37), channel_id=1, source_target_pairs={{0,32},{1,2},{2,1},{3,4},{4,3},{5,6},{6,5},{7,8},{8,7},{9,10},{10,... | collective-permute-start | bytes 3080 | tf_op jit(solution)/shard_map/ppermute | solution.py:539
  3.8 1.4 %copy-start = (f32[2,128,128]{2,1,0:T(8,128)S(1)}, f32[2,128,128]{2,1,0:T(8,128)}, u32[]{:S(2)}) copy-start(f32[2,128,128]{2,1,0:T(8,128)} %load.7) | copy-start | bytes 393220
  4.0 1.2 %collective-permute-start = (f32[2,128]{1,0:T(2,128)S(1)}, f32[2,128]{1,0:T(2,128)S(1)}, u32[]{:S(2)}, u32[]{:S(2)}) collective-permute-start(f32[2,128]{1,0:T(2,128)S(1)} %get-tuple-element.36), channel_id=1, source_target_pairs={{0,1},{1,0},{2,3},{3,2},{4,5},{5,4},{6,7},{7,6},{8,9},{9,8},{10,11... | collective-permute-start | bytes 3080 | tf_op jit(solution)/shard_map/ppermute | solution.py:546
  5.4 4.0 %collective-permute-start.4 = (f32[8,128]{1,0:T(8,128)S(1)}, f32[8,128]{1,0:T(8,128)S(1)}, u32[]{:S(2)}, u32[]{:S(2)}) collective-permute-start(f32[8,128]{1,0:T(8,128)S(1)} %get-tuple-element.42.own), channel_id=1, source_target_pairs={{0,64},{32,96},{64,0},{96,32},{1,65},{33,97},{65,1},{97,33},{2,66}... | collective-permute-start | bytes 12296 | tf_op jit(solution)/shard_map/ppermute | solution.py:511
  8.2 3.7 %collective-permute-start.3 = (f32[8,128]{1,0:T(8,128)S(1)}, f32[8,128]{1,0:T(8,128)S(1)}, u32[]{:S(2)}, u32[]{:S(2)}) collective-permute-start(f32[8,128]{1,0:T(8,128)S(1)} %get-tuple-element.42.own), channel_id=1, source_target_pairs={{0,96},{32,64},{64,32},{96,0},{1,97},{33,65},{65,33},{97,1},{2,98}... | collective-permute-start | bytes 12296 | tf_op jit(solution)/shard_map/ppermute | solution.py:511
  9.1 2.8 %collective-permute-start.2 = (f32[8,128]{1,0:T(8,128)S(1)}, f32[8,128]{1,0:T(8,128)S(1)}, u32[]{:S(2)}, u32[]{:S(2)}) collective-permute-start(f32[8,128]{1,0:T(8,128)S(1)} %get-tuple-element.42.own), channel_id=1, source_target_pairs={{0,32},{32,0},{64,96},{96,64},{1,33},{33,1},{65,97},{97,65},{2,34}... | collective-permute-start | bytes 12296 | tf_op jit(solution)/shard_map/ppermute | solution.py:511
  29.6 4.0 %collective-permute-start.7 = (f32[2,128]{1,0:T(2,128)S(1)}, f32[2,128]{1,0:T(2,128)S(1)}, u32[]{:S(2)}, u32[]{:S(2)}) collective-permute-start(f32[2,128]{1,0:T(2,128)S(1)} %get-tuple-element.53.own), channel_id=1, source_target_pairs={{0,64},{32,96},{64,0},{96,32},{1,65},{33,97},{65,1},{97,33},{2,66}... | collective-permute-start | bytes 3080 | tf_op jit(solution)/shard_map/ppermute | solution.py:511
  30.9 3.9 %collective-permute-start.6 = (f32[2,128]{1,0:T(2,128)S(1)}, f32[2,128]{1,0:T(2,128)S(1)}, u32[]{:S(2)}, u32[]{:S(2)}) collective-permute-start(f32[2,128]{1,0:T(2,128)S(1)} %get-tuple-element.53.own), channel_id=1, source_target_pairs={{0,96},{32,64},{64,32},{96,0},{1,97},{33,65},{65,33},{97,1},{2,98}... | collective-permute-start | bytes 3080 | tf_op jit(solution)/shard_map/ppermute | solution.py:511
  31.7 3.0 %collective-permute-start.5 = (f32[2,128]{1,0:T(2,128)S(1)}, f32[2,128]{1,0:T(2,128)S(1)}, u32[]{:S(2)}, u32[]{:S(2)}) collective-permute-start(f32[2,128]{1,0:T(2,128)S(1)} %get-tuple-element.53.own), channel_id=1, source_target_pairs={{0,32},{32,0},{64,96},{96,64},{1,33},{33,1},{65,97},{97,65},{2,34}... | collective-permute-start | bytes 3080 | tf_op jit(solution)/shard_map/ppermute | solution.py:511
